TPU v7x, 512 devices: a whole 4x4x16 slice. The times are simulated.
512 devices in a mesh: expert: 32 (over z, x_lo), fsdp: 16 (over x_hi, y, core).
Axes of the slice: x: 4 (x_hi: 2, x_lo: 2; x = x_hi * 2 + x_lo), y: 4, z: 16, core: 2. Of those that a mesh axis runs over, the one named last changes fastest.
Arguments:
- tokens: bfloat16 [3584, 4096], P(('expert', 'fsdp')), may hold values from -6 to 6
- expert_ids: int32 [3584, 8], P(('expert', 'fsdp')), may hold values from 0 to 31, all different within a row; in each aligned block of 7 rows (0 to 6, 7 to 13, ...) at most 2 rows name the same one
- gate_scores: float32 [3584, 8], P(('expert', 'fsdp')), may hold values from 0.05 to 1
- w_gate: bfloat16 [32, 1536, 4096], P('expert', 'fsdp'), may hold values from -0.09375 to 0.09375
- w_up: bfloat16 [32, 1536, 4096], P('expert', 'fsdp'), may hold values from -0.09375 to 0.09375
- w_down: bfloat16 [32, 1536, 4096], P('expert', None, 'fsdp'), may hold values from -0.15625 to 0.15625
Outputs:
- mixed: bfloat16 [3584, 4096], P(('expert', 'fsdp'))
Inputs may be any that keep to these rules, and one draw needn't show every extreme that they name: `expert_ids`: each token names 8 different experts. Within the 7 tokens of one device (aligned blocks of rows) no expert is named more than 2 times, and in every draw some expert is named exactly 2 times in some block.
All inputs are finite; a program needn't handle non-finite values.
Results may differ from a plain program's by a relative error of at most 0.0057.
Values may be sent and summed in bfloat16 or wider, within the bound.
A program may use at most 64 MiB of HBM per device.

v0:
```python
import jax
import jax.numpy as jnp
from jax import lax
from jax.sharding import PartitionSpec as P


def on_device(tokens, expert_ids, gate_scores, w_gate, w_up, w_down):
    n_expert = lax.axis_size("expert")
    n_fsdp = lax.axis_size("fsdp")
    local_tok, top_k = expert_ids.shape
    per_column = w_gate.shape[0]
    experts = per_column * n_expert
    capacity = min(local_tok, max(2, 3 * local_tok * top_k // (2 * experts)))
    width = tokens.shape[1]
    feature_cols = w_down.shape[2]
    weights = gate_scores / jnp.sum(gate_scores, axis=1, keepdims=True)
    expert_iota = lax.broadcasted_iota(jnp.int32, (1, 1, experts), 2)
    matches = (expert_ids[:, :, None] == expert_iota).astype(jnp.int32)
    chosen = jnp.sum(matches, axis=1, dtype=jnp.int32)
    weight_table = jnp.sum(weights[:, :, None] * matches.astype(jnp.float32), axis=1)
    ranks = jnp.cumsum(chosen, axis=0, dtype=jnp.int32) - chosen
    slot_iota = lax.broadcasted_iota(jnp.int32, (1, 1, capacity), 2)
    slot_mask = jnp.logical_and(ranks[:, :, None] == slot_iota, chosen[:, :, None] > 0)
    select_f32 = jnp.transpose(slot_mask.astype(jnp.float32), (1, 2, 0))
    select_bf = select_f32.astype(jnp.bfloat16)
    combine_table = select_f32 * jnp.transpose(weight_table)[:, None, :]
    outgoing = jnp.einsum("ect,td->ecd", select_bf, tokens, preferred_element_type=jnp.float32)
    outgoing = outgoing.astype(jnp.bfloat16)
    arrived = lax.all_to_all(outgoing, "expert", split_axis=0, concat_axis=0, tiled=True)
    portion = lax.all_gather(arrived[None], "fsdp", axis=0, tiled=True)
    routed = portion.reshape(portion.shape[0], n_expert, per_column, capacity, width)
    gate_act = jnp.einsum("knjcd,jhd->knjch", routed, w_gate, preferred_element_type=jnp.float32)
    up_act = jnp.einsum("knjcd,jhd->knjch", routed, w_up, preferred_element_type=jnp.float32)
    hidden = (jax.nn.silu(gate_act) * up_act).astype(jnp.bfloat16)
    summed = jnp.einsum(
        "fnjch,jhd->fnjcd",
        lax.all_gather(hidden, "fsdp", axis=4, tiled=True),
        w_down,
        preferred_element_type=jnp.float32,
    )
    expert_out = summed.astype(jnp.bfloat16).reshape(
        n_fsdp, n_expert, per_column * capacity, feature_cols
    )
    returned = lax.all_to_all(
        lax.all_to_all(expert_out, "expert", split_axis=1, concat_axis=1, tiled=True),
        "fsdp",
        split_axis=0,
        concat_axis=3,
        tiled=True,
    )
    returned = returned.reshape(experts, capacity, width)
    mixed = jnp.einsum(
        "ect,ecd->td", combine_table, returned.astype(jnp.float32), precision=lax.Precision.HIGHEST
    )
    return mixed.astype(jnp.bfloat16)


def solution(mesh):
    placed = (
        P(("expert", "fsdp"), None),
        P(("expert", "fsdp"), None),
        P(("expert", "fsdp"), None),
        P("expert", "fsdp", None),
        P("expert", "fsdp", None),
        P("expert", None, "fsdp"),
    )
    return jax.shard_map(
        on_device,
        mesh=mesh,
        in_specs=placed,
        out_specs=P(("expert", "fsdp"), None),
        check_vma=False,
    )
```

profile of v0, /device:TPU:1, one launch (start us, length us, event | category | flops | bytes accessed | tf_op | source)
XLA Modules:
  0.0 343.0 jit_solution(12220957122521888835)
XLA Ops:
  6.5 0.0 copy-start
  6.5 0.0 all-gather.6.cloned.1.call-start
  6.5 0.8 convert_reduce_fusion
  7.4 1.2 convolution_convert_fusion
  8.6 0.5 copy.34
  9.2 48.1 %all_to_all.25 = bf16[32,2,4096]{2,1,0:T(2,128)(2,1)S(1)} all-to-all(bf16[32,2,4096]{2,1,0:T(2,128)(2,1)S(1)} %copy.34), channel_id=1, replica_groups=mesh['expert'=32,'fsdp'=16] {'expert'}, dimensions={0} | all-to-all | bytes 1048576 | tf_op jit(solution)/shard_map/all_to_all | solution.py:29
  57.3 1.1 copy.35
  58.4 0.0 all-gather.6.cloned.1.call-update
  58.4 0.0 all-gather.4.cloned.1.call-start
  58.5 82.3 %all-gather.6.cloned.1.call-done = bf16[512,2,4096]{2,0,1:T(8,128)(2,1)} async-done(((bf16[32,2,4096]{2,0,1:T(8,128)(2,1)}), bf16[512,2,4096]{2,0,1:T(8,128)(2,1)}) %all-gather.6.cloned.1.call-update) | async-done | bytes 8388624 | tf_op jit(solution)/shard_map/all_gather | solution.py:30
  140.8 0.0 copy-start.3
  140.8 0.0 copy-start.4
  140.8 6.0 %fusion.10 = f32[16,32,1,2,96]{4,1,3,0,2:T(8,128)S(1)} fusion(bf16[16,32,2,4096]{3,1,0,2:T(8,128)(2,1)} %bitcast.65, bf16[1,96,4096]{2,1,0:T(8,128)(2,1)} %param.9), kind=kOutput, calls=%fused_computation.10 | convolution fusion | flops 805306368 | bytes 9568256 | tf_op jit(solution)/shard_map/knjcd,jhd->knjch/dot_general | solution.py:32
  146.8 0.0 copy-done.3
  146.8 0.1 copy-done.4
  146.9 2.3 fusion.19
  149.3 2.1 copy.38
  151.3 0.0 all-gather.4.cloned.1.call-update
  151.4 103.8 %all-gather.4.cloned.1.call-done = bf16[16,32,1,2,1536]{1,0,3,2,4:T(8,128)(2,1)} async-done(((bf16[16,32,1,2,96]{1,0,3,2,4:T(8,128)(2,1)}), bf16[16,32,1,2,1536]{1,0,3,2,4:T(8,128)(2,1)}) %all-gather.4.cloned.1.call-update) | async-done | bytes 3145744 | tf_op jit(solution)/shard_map/all_gather | solution.py:37
  255.2 13.4 %copy.39 = bf16[16,32,1,2,1536]{4,1,3,0,2:T(8,128)(2,1)} copy(bf16[16,32,1,2,1536]{1,0,3,2,4:T(8,128)(2,1)} %all-gather.4.cloned.1.call-done) | data formatting | bytes 6291456 | tf_op jit(solution)/shard_map/all_gather | solution.py:37
  268.6 0.0 copy-done
  268.6 0.0 copy-start.2
  268.6 0.0 copy-start.1
  268.6 2.9 fusion.7
  271.5 0.5 copy.40
  272.0 44.3 %all_to_all.26 = bf16[16,32,2,256]{3,2,0,1:T(2,128)(2,1)S(1)} all-to-all(bf16[16,32,2,256]{3,2,0,1:T(2,128)(2,1)S(1)} %copy.40), channel_id=1, replica_groups=mesh['expert'=32,'fsdp'=16] {'expert'}, dimensions={1} | all-to-all | bytes 1048576 | tf_op jit(solution)/shard_map/all_to_all | solution.py:45
  316.4 1.3 copy.41
  317.7 5.8 %all-to-all-start.2 = ((bf16[16,32,2,256]{3,2,1,0:T(2,128)(2,1)}), bf16[16,32,2,256]{3,2,1,0:T(2,128)(2,1)S(1)}, u32[]{:S(2)}, u32[]{:S(2)}) async-start(bf16[16,32,2,256]{3,2,1,0:T(2,128)(2,1)} %copy.41), calls=%async_computation.2 | async-start | bytes 1048576 | tf_op jit(solution)/shard_map/all_to_all | solution.py:44
  323.4 0.0 copy-done.2
  323.4 0.1 reduce_sum.28
  323.6 0.1 broadcast_divide_fusion
  323.6 0.0 copy-done.1
  323.6 0.1 fusion.27
  323.7 10.9 %all-to-all-done.2 = bf16[16,32,2,256]{3,2,1,0:T(2,128)(2,1)S(1)} async-done(((bf16[16,32,2,256]{3,2,1,0:T(2,128)(2,1)}), bf16[16,32,2,256]{3,2,1,0:T(2,128)(2,1)S(1)}, u32[]{:S(2)}, u32[]{:S(2)}) %all-to-all-start.2) | async-done | bytes 524320 | tf_op jit(solution)/shard_map/all_to_all | solution.py:44
  334.6 0.3 copy.42
  334.9 0.2 reshape.47
  335.2 1.0 fusion.4
  (3 shorter events, 0.0 us)
Async XLA Ops:
  6.5 262.1 %copy-start = (bf16[1,1536,256]{2,1,0:T(8,128)(2,1)S(1)}, bf16[1,1536,256]{2,1,0:T(8,128)(2,1)}, u32[]{:S(2)}) copy-start(bf16[1,1536,256]{2,1,0:T(8,128)(2,1)} %param.11) | copy-start | bytes 2359300
  6.5 134.3 %all-gather.6.cloned.1.call-start = ((), (), s32[]{:S(2)}) async-start(), calls=%async_computation.4 | async-start | bytes 8912896 | tf_op jit(solution)/shard_map/all_gather | solution.py:30
  58.4 196.7 %all-gather.4.cloned.1.call-start = ((), (), s32[]{:S(2)}) async-start(), calls=%async_computation.3 | async-start | bytes 13369344 | tf_op jit(solution)/shard_map/all_gather | solution.py:37
  140.8 6.0 %copy-start.3 = (bf16[512,2,4096]{2,0,1:T(8,128)(2,1)S(1)}, bf16[512,2,4096]{2,0,1:T(8,128)(2,1)}, u32[]{:S(2)}) copy-start(bf16[512,2,4096]{2,0,1:T(8,128)(2,1)} %all-gather.6.cloned.1.call-done) | copy-start | bytes 25165828
  140.8 6.1 %copy-start.4 = (bf16[1,96,4096]{2,1,0:T(8,128)(2,1)S(1)}, bf16[1,96,4096]{2,1,0:T(8,128)(2,1)}, u32[]{:S(2)}) copy-start(bf16[1,96,4096]{2,1,0:T(8,128)(2,1)} %param.10) | copy-start | bytes 2359300
  268.6 54.9 %copy-start.2 = (f32[7,8]{1,0:T(8,128)S(1)}, f32[7,8]{1,0:T(8,128)}, u32[]{:S(2)}) copy-start(f32[7,8]{1,0:T(8,128)} %param.8) | copy-start | bytes 676
  268.6 55.1 %copy-start.1 = (s32[7,8]{1,0:T(8,128)S(1)}, s32[7,8]{1,0:T(8,128)}, u32[]{:S(2)}) copy-start(s32[7,8]{1,0:T(8,128)} %param.7) | copy-start | bytes 676
  317.7 16.9 %all-to-all-start.2 = ((bf16[16,32,2,256]{3,2,1,0:T(2,128)(2,1)}), bf16[16,32,2,256]{3,2,1,0:T(2,128)(2,1)S(1)}, u32[]{:S(2)}, u32[]{:S(2)}) async-start(bf16[16,32,2,256]{3,2,1,0:T(2,128)(2,1)} %copy.41), calls=%async_computation.2 | async-start | bytes 1048576 | tf_op jit(solution)/shard_map/all_to_all | solution.py:44
Sparse Core Ops, SparseCore 0:
  58.6 82.1 all-gather.5
  151.5 103.6 all-gather.3
where the time goes:
time: 344 us; the launch traced here: 343 us
  waiting for transfers between devices  197 us (57%)
  blocking collectives  92.5 us (27%)
  local copies, waits for them, and re-layouts  19.6 us (6%)
  between operations  13.5 us (4%)
  matrix products  13.4 us (4%)
  starting transfers between devices  5.81 us (2%)
    all_gather x1, waiting for transfers between devices, on_device(): lax.all_gather(hidden, 'fsdp', axis=4, tiled=True)  104 us
    all_gather x1, waiting for transfers between devices, on_device(): portion = lax.all_gather(arrived[None], 'fsdp', axis=0, tiled=True)  82.3 us
    all_to_all x1, blocking collectives, on_device(): lax.all_to_all(outgoing, 'expert', split_axis=0, concat_axis=0, tiled=True)  48.1 us
    all_to_all x1, blocking collectives, on_device(): lax.all_to_all(expert_out, 'expert', split_axis=1, concat_axis=1, tiled=T...  44.3 us
    all_gather x1, local copies, waits for them, and re-layouts, on_device(): lax.all_gather(hidden, 'fsdp', axis=4, tiled=True)  13.4 us
    all_to_all x1, waiting for transfers between devices, on_device(): lax.all_to_all(lax.all_to_all(expert_out, 'expert', split_axis=1, concat_...  10.9 us
  transfers between devices with their start and end apart: 3, of which 3 were waited for; matrix products, arithmetic and copies ran while one was open for 0% of the time, Pallas kernels for 0%

commit v1 on v0

v1 whole, which is shorter than its diff:
```python
import functools

import jax
import jax.numpy as jnp
from jax import lax
from jax.experimental import pallas as pl
from jax.experimental.pallas import tpu as pltpu
from jax.sharding import PartitionSpec as P

MESH = pl.DeviceIdType.MESH
ANY = pl.BlockSpec(memory_space=pl.ANY)


def offset_of(i, n):
    return n // 2 + ((i % 2) * 2 - 1) * ((i + 1) // 2)


def greet_all(axis, n):
    me = lax.axis_index(axis)
    barrier = pltpu.get_barrier_semaphore()

    def greet(i, carry):
        partner = lax.rem(me + i, n)
        pl.semaphore_signal(barrier, inc=1, device_id={axis: partner}, device_id_type=MESH)
        return carry

    lax.fori_loop(1, n, greet, 0)
    pl.semaphore_wait(barrier, n - 1)


def exchange_kernel(axis, n, x_ref, y_ref, send_sem, recv_sem, own_sem):
    me = lax.axis_index(axis)
    greet_all(axis, n)

    def copy(i, source, target, slot):
        return pltpu.make_async_remote_copy(
            src_ref=x_ref.at[source],
            dst_ref=y_ref.at[slot],
            send_sem=send_sem.at[i],
            recv_sem=recv_sem.at[i],
            device_id={axis: target},
            device_id_type=MESH,
        )

    def send(i, carry):
        partner = lax.rem(me + offset_of(i, n), n)
        copy(i, partner, partner, me).start()
        return carry

    lax.fori_loop(0, n - 1, send, 0)
    own = pltpu.make_async_copy(x_ref.at[me], y_ref.at[me], own_sem)
    own.start()

    def finish(i, carry):
        partner = lax.rem(me + offset_of(i, n), n)
        origin = lax.rem(me - offset_of(i, n) + n, n)
        done = copy(i, partner, partner, origin)
        done.wait_recv()
        done.wait_send()
        return carry

    lax.fori_loop(0, n - 1, finish, 0)
    own.wait()


def exchange(x, axis, n, number):
    return pl.pallas_call(
        functools.partial(exchange_kernel, axis, n),
        out_shape=jax.ShapeDtypeStruct(x.shape, x.dtype),
        in_specs=[ANY],
        out_specs=ANY,
        scratch_shapes=[
            pltpu.SemaphoreType.DMA((n - 1,)),
            pltpu.SemaphoreType.DMA((n - 1,)),
            pltpu.SemaphoreType.DMA,
        ],
        compiler_params=pltpu.CompilerParams(collective_id=number, has_side_effects=True),
    )(x)


def columns_kernel(axis, n, x_ref, y_ref, send_sem, recv_sem, own_sem):
    me = lax.axis_index(axis)
    width = x_ref.shape[2]
    greet_all(axis, n)

    def place(block):
        return y_ref.at[:, pl.ds(pl.multiple_of(block * width, width), width)]

    def copy(i, target, slot):
        return pltpu.make_async_remote_copy(
            src_ref=x_ref.at[target],
            dst_ref=place(slot),
            send_sem=send_sem.at[i],
            recv_sem=recv_sem.at[i],
            device_id={axis: target},
            device_id_type=MESH,
        )

    def send(i, carry):
        copy(i, lax.rem(me + offset_of(i, n), n), me).start()
        return carry

    lax.fori_loop(0, n - 1, send, 0)
    own = pltpu.make_async_copy(x_ref.at[me], place(me), own_sem)
    own.start()

    def finish(i, carry):
        partner = lax.rem(me + offset_of(i, n), n)
        origin = lax.rem(me - offset_of(i, n) + n, n)
        done = copy(i, partner, origin)
        done.wait_recv()
        done.wait_send()
        return carry

    lax.fori_loop(0, n - 1, finish, 0)
    own.wait()


def to_columns(x, axis, n, number):
    return pl.pallas_call(
        functools.partial(columns_kernel, axis, n),
        out_shape=jax.ShapeDtypeStruct((x.shape[1], n * x.shape[2]), x.dtype),
        in_specs=[pl.BlockSpec(memory_space=pltpu.VMEM)],
        out_specs=ANY,
        scratch_shapes=[
            pltpu.SemaphoreType.DMA((n - 1,)),
            pltpu.SemaphoreType.DMA((n - 1,)),
            pltpu.SemaphoreType.DMA,
        ],
        compiler_params=pltpu.CompilerParams(collective_id=number, has_side_effects=True),
    )(x)


def gather_kernel(x_ref, y_ref, send_sem, recv_sem, own_sem):
    me = lax.axis_index("fsdp")
    core, yy, xh = me % 2, (me // 2) % 4, me // 8
    half = x_ref.shape[0] // 2

    def index(h, y, c):
        return (h * 4 + y) * 2 + c

    up, down, far = (yy + 1) % 4, (yy + 3) % 4, (yy + 2) % 4
    other = 1 - xh
    to_up, to_down = index(xh, up, core), index(xh, down, core)
    to_x, to_core = index(other, yy, core), index(xh, yy, 1 - core)

    barrier = pltpu.get_barrier_semaphore()
    for partner in (to_up, to_down, to_x, to_core):
        pl.semaphore_signal(barrier, inc=1, device_id={"fsdp": partner}, device_id_type=MESH)
    pl.semaphore_wait(barrier, 4)

    sent = []

    def place(block, piece):
        return y_ref.at[block, pl.ds(piece * half, half)]

    def send(block, piece, target, own=False):
        copy = pltpu.make_async_remote_copy(
            src_ref=x_ref.at[pl.ds(piece * half, half)] if own else place(block, piece),
            dst_ref=place(block, piece),
            send_sem=send_sem.at[len(sent)],
            recv_sem=recv_sem.at[block, piece],
            device_id={"fsdp": target},
            device_id_type=MESH,
        )
        copy.start()
        sent.append(copy)

    def arrived(block, piece):
        pltpu.make_async_remote_copy(
            src_ref=place(block, piece),
            dst_ref=place(block, piece),
            send_sem=send_sem.at[0],
            recv_sem=recv_sem.at[block, piece],
            device_id={"fsdp": to_core},
            device_id_type=MESH,
        ).wait_recv()

    for piece in (0, 1):
        send(me, piece, to_x, True)
        send(me, piece, to_up, True)
        send(me, 1 - piece, to_down, True)
        send(me, piece, to_core, True)
    own = pltpu.make_async_copy(x_ref, y_ref.at[me], own_sem)
    own.start()

    def ring_first(h):
        block = index(h, down, core)
        arrived(block, 0)
        send(block, 0, to_up)
        send(block, 0, to_core)
        block = index(h, up, core)
        arrived(block, 1)
        send(block, 1, to_down)
        send(block, 1, to_core)

    def ring_rest(h):
        for block, piece in (
            (index(h, down, core), 1),
            (index(h, up, core), 0),
            (index(h, far, core), 0),
            (index(h, far, core), 1),
        ):
            arrived(block, piece)
            send(block, piece, to_core)

    ring_first(xh)
    for piece in (0, 1):
        arrived(to_x, piece)
        send(to_x, piece, to_up)
        send(to_x, piece, to_down)
        send(to_x, piece, to_core)
    ring_rest(xh)
    ring_first(other)
    ring_rest(other)
    for h in (0, 1):
        for y in range(4):
            for piece in (0, 1):
                arrived(index(h, y, 1 - core), piece)
    for copy in sent:
        copy.wait_send()
    own.wait()


def gather(x, number):
    return pl.pallas_call(
        gather_kernel,
        out_shape=jax.ShapeDtypeStruct((16,) + x.shape, x.dtype),
        in_specs=[pl.BlockSpec(memory_space=pltpu.VMEM)],
        out_specs=ANY,
        scratch_shapes=[
            pltpu.SemaphoreType.DMA((30,)),
            pltpu.SemaphoreType.DMA((16, 2)),
            pltpu.SemaphoreType.DMA,
        ],
        compiler_params=pltpu.CompilerParams(collective_id=number, has_side_effects=True),
    )(x)


def on_device(tokens, expert_ids, gate_scores, w_gate, w_up, w_down):
    n_expert = lax.axis_size("expert")
    n_fsdp = lax.axis_size("fsdp")
    local_tok, top_k = expert_ids.shape
    experts = n_expert
    capacity = 2
    width = tokens.shape[1]
    feature_cols = w_down.shape[2]
    weights = gate_scores / jnp.sum(gate_scores, axis=1, keepdims=True)
    expert_iota = lax.broadcasted_iota(jnp.int32, (1, 1, experts), 2)
    matches = (expert_ids[:, :, None] == expert_iota).astype(jnp.int32)
    chosen = jnp.sum(matches, axis=1, dtype=jnp.int32)
    weight_table = jnp.sum(weights[:, :, None] * matches.astype(jnp.float32), axis=1)
    ranks = jnp.cumsum(chosen, axis=0, dtype=jnp.int32) - chosen
    slot_iota = lax.broadcasted_iota(jnp.int32, (1, 1, capacity), 2)
    slot_mask = jnp.logical_and(ranks[:, :, None] == slot_iota, chosen[:, :, None] > 0)
    select_f32 = jnp.transpose(slot_mask.astype(jnp.float32), (1, 2, 0))
    select_bf = select_f32.astype(jnp.bfloat16)
    combine_table = select_f32 * jnp.transpose(weight_table)[:, None, :]
    outgoing = jnp.einsum("ect,td->ecd", select_bf, tokens, preferred_element_type=jnp.float32)
    outgoing = outgoing.astype(jnp.bfloat16)
    arrived = exchange(outgoing, "expert", n_expert, 0)
    routed = gather(arrived.reshape(experts * capacity, width), 1)
    routed = routed.reshape(n_fsdp * experts * capacity, width)
    contract = (((1,), (1,)), ((), ()))
    gate_act = lax.dot_general(w_gate[0], routed, contract, preferred_element_type=jnp.float32)
    up_act = lax.dot_general(w_up[0], routed, contract, preferred_element_type=jnp.float32)
    hidden = (jax.nn.silu(gate_act) * up_act).astype(jnp.bfloat16)
    hidden = gather(hidden, 2)
    hidden = hidden.reshape(w_down.shape[1], hidden.shape[2])
    summed = lax.dot_general(
        hidden, w_down[0], (((0,), (0,)), ((), ())), preferred_element_type=jnp.float32
    )
    expert_out = summed.astype(jnp.bfloat16).reshape(n_fsdp, experts * capacity, feature_cols)
    rows = to_columns(expert_out, "fsdp", n_fsdp, 3)
    returned = exchange(rows.reshape(experts, capacity, width), "expert", n_expert, 4)
    mixed = jnp.einsum(
        "ect,ecd->td", combine_table, returned.astype(jnp.float32), precision=lax.Precision.HIGHEST
    )
    return mixed.astype(jnp.bfloat16)


def solution(mesh):
    placed = (
        P(("expert", "fsdp"), None),
        P(("expert", "fsdp"), None),
        P(("expert", "fsdp"), None),
        P("expert", "fsdp", None),
        P("expert", "fsdp", None),
        P("expert", None, "fsdp"),
    )
    return jax.shard_map(
        on_device,
        mesh=mesh,
        in_specs=placed,
        out_specs=P(("expert", "fsdp"), None),
        check_vma=False,
    )
```

time: 344 us -> 179 us (0.52)
  waiting for transfers between devices: 197 us -> 0 us
  Pallas kernels: 0 us -> 154 us
  blocking collectives: 92.5 us -> 0 us
  local copies, waits for them, and re-layouts: 19.6 us -> 5.65 us
  between operations: 13.5 us -> 0.13 us
  starting transfers between devices: 5.81 us -> 0 us
    all_gather x2 -> x0, waiting for transfers between devices: 186 us -> none  [the longest x1 104 us: on_device(): lax.all_gather(hidden, 'fsdp', axis=4, tiled=True)]
    pallas_call x0 -> x5, Pallas kernels: none -> 154 us  [the longest x2 71.9 us: exchange(): pl.pallas_call(functools.partial(exchange_kernel, axis, n), out_shape=jax...]
    all_to_all x2 -> x0, blocking collectives: 92.5 us -> none  [the longest x1 48.1 us: on_device(): lax.all_to_all(outgoing, 'expert', split_axis=0, concat_axis=0, tiled=True)]
    all_gather x1 -> x0, local copies, waits for them, and re-layouts: 13.4 us -> none  [on_device(): lax.all_gather(hidden, 'fsdp', axis=4, tiled=True)]
    all_to_all x1 -> x0, waiting for transfers between devices: 10.9 us -> none  [on_device(): lax.all_to_all(lax.all_to_all(expert_out, 'expert', split_axis=1, concat_...]
    all_to_all x1 -> x0, starting transfers between devices: 5.77 us -> none  [on_device(): lax.all_to_all(lax.all_to_all(expert_out, 'expert', split_axis=1, concat_...]
    reshape x1 -> x2, local copies, waits for them, and re-layouts: 0.24 us -> 4.27 us  [the longest x1 2.19 us: on_device(): rows.reshape(experts, capacity, width)]
  transfers between devices with their start and end apart: 3 -> 0, of which waited for: 3 -> 0; matrix products, arithmetic and copies ran while one was open for 0% -> 0% of each run, Pallas kernels for 0% -> 0%
where the time goes in v1:
time: 179 us; the launch traced here: 177 us
  Pallas kernels  154 us (86%)
  matrix products  16.8 us (9%)
  local copies, waits for them, and re-layouts  5.65 us (3%)
    pallas_call x2, Pallas kernels, exchange(): pl.pallas_call(functools.partial(exchange_kernel, axis, n), out_shape=jax...  71.9 us
    pallas_call x2, Pallas kernels, gather(): pl.pallas_call(gather_kernel, out_shape=jax.ShapeDtypeStruct((16,) + x.sh...  67.3 us
    pallas_call x1, Pallas kernels, to_columns(): pl.pallas_call(functools.partial(columns_kernel, axis, n), out_shape=jax....  14.3 us
    dot_general x1, matrix products, on_device(): lax.dot_general(w_gate[0], routed, contract, preferred_element_type=jnp.f...  6.22 us
    dot_general x1, matrix products, on_device(): lax.dot_general(hidden, w_down[0], (((0,), (0,)), ((), ())), preferred_el...  3.7 us

profile of v1, /device:TPU:1, one launch (start us, length us, event | category | flops | bytes accessed | tf_op | source)
XLA Modules:
  0.0 177.4 jit_solution(10821991284452271973)
XLA Ops:
  0.0 0.0 copy-start
  0.0 0.0 copy-start.2
  0.0 0.9 convert_reduce_fusion
  0.9 1.2 fusion.7
  2.1 1.4 copy.14.x_ref
  3.5 40.9 %shard_map.64 = bf16[32,2,4096]{2,1,0:T(2,128)(2,1)} custom-call(bf16[32,2,4096]{2,1,0:T(2,128)(2,1)} %copy.14.x_ref), custom_call_target="tpu_custom_call" | custom-call | tf_op jit(solution)/shard_map/pallas_call | solution.py:67
  44.4 2.1 %reshape.32.x_ref = bf16[64,4096]{1,0:T(8,128)(2,1)} reshape(bf16[32,2,4096]{2,1,0:T(2,128)(2,1)} %shard_map.64) | data formatting | bytes 1048576 | tf_op jit(solution)/shard_map/reshape | solution.py:262
  46.5 0.0 copy-start.5
  46.5 45.1 %shard_map.65 = bf16[16,64,4096]{2,1,0:T(8,128)(2,1)} custom-call(bf16[64,4096]{1,0:T(8,128)(2,1)} %reshape.32.x_ref), custom_call_target="tpu_custom_call" | custom-call | tf_op jit(solution)/shard_map/pallas_call | solution.py:226
  91.6 0.0 copy-start.1
  91.6 0.0 copy-done.2
  91.6 6.2 %convolution_bitcast_fusion.2 = f32[96,1024]{1,0:T(8,128)S(1)} fusion(bf16[1024,4096]{1,0:T(8,128)(2,1)} %bitcast.35, bf16[1,96,4096]{2,1,0:T(8,128)(2,1)S(1)} %copy-done.2), kind=kOutput, calls=%fused_computation.5 | convolution fusion | flops 805306368 | bytes 9568256 | tf_op jit(solution)/shard_map/dot_general | solution.py:265
  97.8 0.0 copy-done.5
  97.9 0.0 copy-done.1
  97.9 3.5 %fusion.2.x_ref = bf16[96,1024]{1,0:T(8,128)(2,1)} fusion(bf16[1024,4096]{1,0:T(8,128)(2,1)S(1)} %bitcast.36, bf16[1,96,4096]{2,1,0:T(8,128)(2,1)S(1)} %copy-done.5, f32[96,1024]{1,0:T(8,128)S(1)} %convolution_bitcast_fusion.2), kind=kOutput, calls=%fused_computation.6 | convolution fusion | flops 805896192 | bytes 9764864 | tf_op jit(solution)/shard_map/dot_general | solution.py:266
  101.3 0.0 copy-start.4
  101.3 0.0 copy-start.3
  101.3 22.2 %shard_map.66 = bf16[16,96,1024]{2,1,0:T(8,128)(2,1)} custom-call(bf16[96,1024]{1,0:T(8,128)(2,1)} %fusion.2.x_ref), custom_call_target="tpu_custom_call" | custom-call | tf_op jit(solution)/shard_map/pallas_call | solution.py:226
  123.6 0.0 copy-done
  123.6 3.7 %convolution_convert_fusion = bf16[1024,256]{1,0:T(8,128)(2,1)} fusion(bf16[1536,1024]{1,0:T(8,128)(2,1)} %bitcast.37, bf16[1,1536,256]{2,1,0:T(8,128)(2,1)S(1)} %copy-done), kind=kOutput, calls=%fused_computation.2 | convolution fusion | flops 805568512 | bytes 4456448 | tf_op jit(solution)/shard_map/dot_general | solution.py:270
  127.3 14.3 %shard_map.67 = bf16[64,4096]{1,0:T(8,128)(2,1)} custom-call(bf16[16,64,256]{2,1,0:T(8,128)(2,1)} %bitcast.38), custom_call_target="tpu_custom_call" | custom-call | tf_op jit(solution)/shard_map/pallas_call | solution.py:120
  141.6 2.2 %reshape.36.x_ref = bf16[32,2,4096]{2,1,0:T(2,128)(2,1)} reshape(bf16[64,4096]{1,0:T(8,128)(2,1)} %shard_map.67) | data formatting | bytes 1048576 | tf_op jit(solution)/shard_map/reshape | solution.py:275
  143.8 31.1 %shard_map.68 = bf16[32,2,4096]{2,1,0:T(2,128)(2,1)} custom-call(bf16[32,2,4096]{2,1,0:T(2,128)(2,1)} %reshape.36.x_ref), custom_call_target="tpu_custom_call" | custom-call | tf_op jit(solution)/shard_map/pallas_call | solution.py:67
  174.8 0.0 copy-done.4
  174.9 0.1 reduce_sum.28
  175.0 0.1 broadcast_divide_fusion
  175.1 0.0 copy-done.3
  175.1 0.1 fusion.10
  175.2 2.2 %fusion = bf16[7,4096]{1,0:T(8,128)(2,1)} fusion(bf16[32,2,4096]{2,1,0:T(2,128)(2,1)} %shard_map.68, f32[32,7]{0,1:T(8,128)S(1)} %bitcast.39, s32[32,7]{0,1:T(8,128)S(1)} %subtract_bitcast_fusion, pred[32,7]{0,1:T(8,128)(4,1)S(1)} %compare_bitcast_fusion), kind=kOutput, calls=%fused_computation.1 | convolution fusion | flops 22050112 | bytes 583648 | tf_op jit(solution)/shard_map/ect,ecd->td/dot_general | solution.py:276
  (3 shorter events, 0.0 us)
Async XLA Ops:
  0.0 123.6 %copy-start = (bf16[1,1536,256]{2,1,0:T(8,128)(2,1)S(1)}, bf16[1,1536,256]{2,1,0:T(8,128)(2,1)}, u32[]{:S(2)}) copy-start(bf16[1,1536,256]{2,1,0:T(8,128)(2,1)} %param.11) | copy-start | bytes 2359300
  0.0 91.6 %copy-start.2 = (bf16[1,96,4096]{2,1,0:T(8,128)(2,1)S(1)}, bf16[1,96,4096]{2,1,0:T(8,128)(2,1)}, u32[]{:S(2)}) copy-start(bf16[1,96,4096]{2,1,0:T(8,128)(2,1)} %param.9) | copy-start | bytes 2359300
  46.5 51.4 %copy-start.5 = (bf16[1,96,4096]{2,1,0:T(8,128)(2,1)S(1)}, bf16[1,96,4096]{2,1,0:T(8,128)(2,1)}, u32[]{:S(2)}) copy-start(bf16[1,96,4096]{2,1,0:T(8,128)(2,1)} %param.10) | copy-start | bytes 2359300
  91.6 6.3 %copy-start.1 = (bf16[16,64,4096]{2,1,0:T(8,128)(2,1)S(1)}, bf16[16,64,4096]{2,1,0:T(8,128)(2,1)}, u32[]{:S(2)}) copy-start(bf16[16,64,4096]{2,1,0:T(8,128)(2,1)} %shard_map.65) | copy-start | bytes 25165828
  101.3 73.5 %copy-start.4 = (f32[7,8]{1,0:T(8,128)S(1)}, f32[7,8]{1,0:T(8,128)}, u32[]{:S(2)}) copy-start(f32[7,8]{1,0:T(8,128)} %param.8) | copy-start | bytes 676
  101.3 73.7 %copy-start.3 = (s32[7,8]{1,0:T(8,128)S(1)}, s32[7,8]{1,0:T(8,128)}, u32[]{:S(2)}) copy-start(s32[7,8]{1,0:T(8,128)} %param.7) | copy-start | bytes 676

commit v2 on v1

v2 whole, which is shorter than its diff:
```python
import functools

import jax
import jax.numpy as jnp
from jax import lax
from jax.experimental import pallas as pl
from jax.experimental.pallas import tpu as pltpu
from jax.sharding import PartitionSpec as P

MESH = pl.DeviceIdType.MESH
ANY = pl.BlockSpec(memory_space=pl.ANY)
DMA = pltpu.SemaphoreType.DMA
SLOTS = 2
YS = 4
GROUPS = 4


def fsdp_index(xh, y, core):
    return (xh * YS + y) * 2 + core


def fsdp_place():
    me = lax.axis_index("fsdp")
    return me, me // (2 * YS), (me // 2) % YS, me % 2


def settings(number):
    return pltpu.CompilerParams(
        collective_id=number, has_side_effects=True, vmem_limit_bytes=VMEM
    )


VMEM = 4 * 1024 * 1024


def offset_of(i, n):
    return n // 2 + ((i % 2) * 2 - 1) * ((i + 1) // 2)


def greet_all(axis, n, barrier):
    me = lax.axis_index(axis)

    def greet(i, carry):
        partner = lax.rem(me + i, n)
        pl.semaphore_signal(barrier, inc=1, device_id={axis: partner}, device_id_type=MESH)
        return carry

    lax.fori_loop(1, n, greet, 0)


def quarter_kernel(tok_ref, meta_ref, out_ref, info_ref, send_sem, recv_sem, own_sem):
    me, xh, yy, core = fsdp_place()
    quarter = out_ref.shape[2]
    barrier = pltpu.get_barrier_semaphore()
    for k in range(1, YS):
        pl.semaphore_signal(
            barrier,
            inc=1,
            device_id={"fsdp": fsdp_index(xh, (yy + k) % YS, core)},
            device_id_type=MESH,
        )
    pl.semaphore_wait(barrier, YS - 1)

    def part(y):
        return tok_ref.at[:, pl.ds(pl.multiple_of(y * quarter, quarter), quarter)]

    copies = []
    for k in range(1, YS):
        peer = (yy + k) % YS
        target = {"fsdp": fsdp_index(xh, peer, core)}
        for j, (source, place) in enumerate(
            ((part(peer), out_ref.at[yy]), (meta_ref, info_ref.at[yy]))
        ):
            copy = pltpu.make_async_remote_copy(
                src_ref=source,
                dst_ref=place,
                send_sem=send_sem.at[k - 1, j],
                recv_sem=recv_sem.at[k - 1, j],
                device_id=target,
                device_id_type=MESH,
            )
            copy.start()
            copies.append(copy)
    own = [
        pltpu.make_async_copy(part(yy), out_ref.at[yy], own_sem.at[0]),
        pltpu.make_async_copy(meta_ref, info_ref.at[yy], own_sem.at[1]),
    ]
    for copy in own:
        copy.start()
    for k in range(1, YS):
        origin = (yy + YS - k) % YS
        for j, place in enumerate((out_ref.at[origin], info_ref.at[origin])):
            pltpu.make_async_remote_copy(
                src_ref=place,
                dst_ref=place,
                send_sem=send_sem.at[k - 1, j],
                recv_sem=recv_sem.at[k - 1, j],
                device_id={"fsdp": fsdp_index(xh, origin, core)},
                device_id_type=MESH,
            ).wait_recv()
    for copy in copies:
        copy.wait_send()
    for copy in own:
        copy.wait()


def quarters(tok, meta, number):
    rows, width = tok.shape
    vmem = pl.BlockSpec(memory_space=pltpu.VMEM)
    return pl.pallas_call(
        quarter_kernel,
        out_shape=(
            jax.ShapeDtypeStruct((YS, rows, width // YS), tok.dtype),
            jax.ShapeDtypeStruct((YS,) + meta.shape, meta.dtype),
        ),
        in_specs=[vmem, vmem],
        out_specs=(vmem, vmem),
        scratch_shapes=[DMA((YS - 1, 2)), DMA((YS - 1, 2)), DMA((2,))],
        compiler_params=settings(number),
    )(tok, meta)


def dispatch_kernel(n, x_ref, y_ref, a_send, a_recv, send_sem, recv_sem, own_sem):
    e = lax.axis_index("expert")
    me, xh, yy, core = fsdp_place()
    tall, quarter = x_ref.shape[1], x_ref.shape[2]
    size = n // GROUPS
    other = 1 - xh
    up, down, far = (yy + 1) % YS, (yy + YS - 1) % YS, (yy + 2) % YS
    to_up, to_down = fsdp_index(xh, up, core), fsdp_index(xh, down, core)
    to_x, to_core = fsdp_index(other, yy, core), fsdp_index(xh, yy, 1 - core)

    barrier = pltpu.get_barrier_semaphore()
    for partner in (to_up, to_down, to_x, to_core):
        pl.semaphore_signal(barrier, inc=1, device_id={"fsdp": partner}, device_id_type=MESH)
    greet_all("expert", n, barrier)
    pl.semaphore_wait(barrier, n + 3)

    def place(h, y, c, first, count):
        return y_ref.at[
            h * 2 + c,
            pl.ds(pl.multiple_of(first * tall, tall), count * tall),
            pl.ds(pl.multiple_of(y * quarter, quarter), quarter),
        ]

    def hop(i, target):
        return pltpu.make_async_remote_copy(
            src_ref=x_ref.at[target],
            dst_ref=place(xh, yy, core, i, 1),
            send_sem=a_send.at[i],
            recv_sem=a_recv.at[i],
            device_id={"expert": target},
            device_id_type=MESH,
        )

    def launch(i, carry):
        hop(i, lax.rem(e + offset_of(i, n), n)).start()
        return carry

    def land(i, carry):
        hop(i, lax.rem(e + offset_of(i, n), n)).wait_recv()
        return carry

    def clear(i, carry):
        hop(i, lax.rem(e + offset_of(i, n), n)).wait_send()
        return carry

    lax.fori_loop(0, n - 1, launch, 0)
    own = pltpu.make_async_copy(x_ref.at[e], place(xh, yy, core, n - 1, 1), own_sem)
    own.start()

    sent = []

    def copy_of(h, y, c, g, target, slot):
        block = place(h, y, c, g * size, size)
        return pltpu.make_async_remote_copy(
            src_ref=block,
            dst_ref=block,
            send_sem=send_sem.at[slot],
            recv_sem=recv_sem.at[fsdp_index(h, y, c), g],
            device_id={"fsdp": target},
            device_id_type=MESH,
        )

    def send(h, y, g, *targets):
        for target in targets:
            copy = copy_of(h, y, core, g, target, len(sent))
            copy.start()
            sent.append(copy)

    def arrived(h, y, c, g):
        copy_of(h, y, c, g, to_core, 0).wait_recv()

    def from_expert(g):
        lax.fori_loop(g * size, min((g + 1) * size, n - 1), land, 0)
        if g == GROUPS - 1:
            own.wait()
        send(xh, yy, g, to_x, to_up, to_down, to_core)

    def from_x(g):
        arrived(other, yy, core, g)
        send(other, yy, g, to_up, to_down, to_core)

    def from_ring(h, g):
        for y, onward in ((down, to_up), (up, to_down)):
            arrived(h, y, core, g)
            if (g % 2 == 0) == (onward is to_up):
                send(h, y, g, onward)
            send(h, y, g, to_core)

    def from_far(h, g):
        arrived(h, far, core, g)
        send(h, far, g, to_core)

    for step in range(GROUPS + 2):
        if step < GROUPS:
            from_expert(step)
        if 1 <= step <= GROUPS:
            from_x(step - 1)
            from_ring(xh, step - 1)
        if 2 <= step:
            from_far(xh, step - 2)
            from_ring(other, step - 2)
    for g in range(GROUPS):
        from_far(other, g)
    for g in range(GROUPS):
        for h in (0, 1):
            for y in range(YS):
                arrived(h, y, 1 - core, g)
    lax.fori_loop(0, n - 1, clear, 0)
    for copy in sent:
        copy.wait_send()


def dispatch(x, n, number):
    _, tall, quarter = x.shape
    return pl.pallas_call(
        functools.partial(dispatch_kernel, n),
        out_shape=jax.ShapeDtypeStruct((4, n * tall, YS * quarter), x.dtype),
        in_specs=[ANY],
        out_specs=ANY,
        scratch_shapes=[
            DMA((n - 1,)),
            DMA((n - 1,)),
            DMA((15 * GROUPS,)),
            DMA((16, GROUPS)),
            DMA,
        ],
        compiler_params=settings(number),
    )(x)


def collect_kernel(n, m, x_ref, y_ref, rows, f_send, f_recv, a_send, a_recv, own_sem):
    e = lax.axis_index("expert")
    me = lax.axis_index("fsdp")
    width = x_ref.shape[3]
    size = n // GROUPS
    barrier = pltpu.get_barrier_semaphore()
    greet_all("fsdp", m, barrier)
    greet_all("expert", n, barrier)
    pl.semaphore_wait(barrier, n + m - 2)

    def place(first, count, block):
        return rows.at[
            pl.ds(first, count), :, pl.ds(pl.multiple_of(block * width, width), width)
        ]

    def column(i, target, origin):
        g, k = i // (m - 1), i % (m - 1)
        return pltpu.make_async_remote_copy(
            src_ref=x_ref.at[target, pl.ds(g * size, size)],
            dst_ref=place(g * size, size, origin),
            send_sem=f_send.at[g, k],
            recv_sem=f_recv.at[g, k],
            device_id={"fsdp": target},
            device_id_type=MESH,
        )

    def step_of(i):
        return offset_of(i % (m - 1), m)

    def column_start(i, carry):
        column(i, lax.rem(me + step_of(i), m), me).start()
        return carry

    def column_land(i, carry):
        origin = lax.rem(me - step_of(i) + m, m)
        column(i, origin, origin).wait_recv()
        return carry

    def column_clear(i, carry):
        column(i, lax.rem(me + step_of(i), m), me).wait_send()
        return carry

    own_columns = pltpu.make_async_copy(x_ref.at[me], place(0, n, me), own_sem.at[0])
    own_columns.start()
    lax.fori_loop(0, GROUPS * (m - 1), column_start, 0)
    own_columns.wait()

    def back(i, target, slot):
        return pltpu.make_async_remote_copy(
            src_ref=rows.at[i],
            dst_ref=y_ref.at[slot],
            send_sem=a_send.at[i],
            recv_sem=a_recv.at[i],
            device_id={"expert": target},
            device_id_type=MESH,
        )

    def back_start(i, carry):
        back(i, lax.rem(e - offset_of(i, n) + n, n), e).start()
        return carry

    def back_finish(i, carry):
        origin = lax.rem(e + offset_of(i, n), n)
        done = back(i, origin, origin)
        done.wait_recv()
        done.wait_send()
        return carry

    for g in range(GROUPS):
        lax.fori_loop(g * (m - 1), (g + 1) * (m - 1), column_land, 0)
        lax.fori_loop(g * size, min((g + 1) * size, n - 1), back_start, 0)
    own_rows = pltpu.make_async_copy(rows.at[n - 1], y_ref.at[e], own_sem.at[1])
    own_rows.start()
    lax.fori_loop(0, GROUPS * (m - 1), column_clear, 0)
    lax.fori_loop(0, n - 1, back_finish, 0)
    own_rows.wait()


def collect(x, n, m, number):
    _, _, slots, width = x.shape
    return pl.pallas_call(
        functools.partial(collect_kernel, n, m),
        out_shape=jax.ShapeDtypeStruct((n, slots, m * width), x.dtype),
        in_specs=[ANY],
        out_specs=ANY,
        scratch_shapes=[
            pltpu.VMEM((n, slots, m * width), x.dtype),
            DMA((GROUPS, m - 1)),
            DMA((GROUPS, m - 1)),
            DMA((n - 1,)),
            DMA((n - 1,)),
            DMA((2,)),
        ],
        compiler_params=settings(number),
    )(x)


def gather_kernel(x_ref, y_ref, send_sem, recv_sem, own_sem):
    me = lax.axis_index("fsdp")
    core, yy, xh = me % 2, (me // 2) % 4, me // 8
    half = x_ref.shape[0] // 2

    def index(h, y, c):
        return (h * 4 + y) * 2 + c

    up, down, far = (yy + 1) % 4, (yy + 3) % 4, (yy + 2) % 4
    other = 1 - xh
    to_up, to_down = index(xh, up, core), index(xh, down, core)
    to_x, to_core = index(other, yy, core), index(xh, yy, 1 - core)

    barrier = pltpu.get_barrier_semaphore()
    for partner in (to_up, to_down, to_x, to_core):
        pl.semaphore_signal(barrier, inc=1, device_id={"fsdp": partner}, device_id_type=MESH)
    pl.semaphore_wait(barrier, 4)

    sent = []

    def place(block, piece):
        return y_ref.at[block, pl.ds(piece * half, half)]

    def send(block, piece, target, own=False):
        copy = pltpu.make_async_remote_copy(
            src_ref=x_ref.at[pl.ds(piece * half, half)] if own else place(block, piece),
            dst_ref=place(block, piece),
            send_sem=send_sem.at[len(sent)],
            recv_sem=recv_sem.at[block, piece],
            device_id={"fsdp": target},
            device_id_type=MESH,
        )
        copy.start()
        sent.append(copy)

    def arrived(block, piece):
        pltpu.make_async_remote_copy(
            src_ref=place(block, piece),
            dst_ref=place(block, piece),
            send_sem=send_sem.at[0],
            recv_sem=recv_sem.at[block, piece],
            device_id={"fsdp": to_core},
            device_id_type=MESH,
        ).wait_recv()

    for piece in (0, 1):
        send(me, piece, to_x, True)
        send(me, piece, to_up, True)
        send(me, 1 - piece, to_down, True)
        send(me, piece, to_core, True)
    own = pltpu.make_async_copy(x_ref, y_ref.at[me], own_sem)
    own.start()

    def ring_first(h):
        block = index(h, down, core)
        arrived(block, 0)
        send(block, 0, to_up)
        send(block, 0, to_core)
        block = index(h, up, core)
        arrived(block, 1)
        send(block, 1, to_down)
        send(block, 1, to_core)

    def ring_rest(h):
        for block, piece in (
            (index(h, down, core), 1),
            (index(h, up, core), 0),
            (index(h, far, core), 0),
            (index(h, far, core), 1),
        ):
            arrived(block, piece)
            send(block, piece, to_core)

    ring_first(xh)
    for piece in (0, 1):
        arrived(to_x, piece)
        send(to_x, piece, to_up)
        send(to_x, piece, to_down)
        send(to_x, piece, to_core)
    ring_rest(xh)
    ring_first(other)
    ring_rest(other)
    for h in (0, 1):
        for y in range(4):
            for piece in (0, 1):
                arrived(index(h, y, 1 - core), piece)
    for copy in sent:
        copy.wait_send()
    own.wait()


def gather(x, number):
    return pl.pallas_call(
        gather_kernel,
        out_shape=jax.ShapeDtypeStruct((16,) + x.shape, x.dtype),
        in_specs=[pl.BlockSpec(memory_space=pltpu.VMEM)],
        out_specs=ANY,
        scratch_shapes=[
            pltpu.SemaphoreType.DMA((30,)),
            pltpu.SemaphoreType.DMA((16, 2)),
            pltpu.SemaphoreType.DMA,
        ],
        compiler_params=settings(number),
    )(x)


def route(expert_ids, gate_scores, experts):
    weights = gate_scores / jnp.sum(gate_scores, axis=-1, keepdims=True)
    expert_iota = lax.broadcasted_iota(jnp.int32, (1, 1, experts), 2)
    matches = (expert_ids[:, :, None] == expert_iota).astype(jnp.int32)
    chosen = jnp.sum(matches, axis=1, dtype=jnp.int32)
    weight_table = jnp.sum(weights[:, :, None] * matches.astype(jnp.float32), axis=1)
    return chosen, weight_table


def slots_of(chosen):
    ranks = jnp.cumsum(chosen, axis=-2, dtype=jnp.int32) - chosen
    slot_iota = lax.broadcasted_iota(jnp.int32, (1,) * chosen.ndim + (SLOTS,), chosen.ndim)
    return jnp.logical_and(ranks[..., None] == slot_iota, chosen[..., None] > 0)


def on_device(tokens, expert_ids, gate_scores, w_gate, w_up, w_down):
    n_expert = lax.axis_size("expert")
    n_fsdp = lax.axis_size("fsdp")
    local_tok, top_k = expert_ids.shape
    experts = n_expert
    width = tokens.shape[1]
    feature_cols = w_down.shape[2]
    tall = YS * SLOTS

    chosen, weight_table = route(expert_ids, gate_scores, experts)
    select = jnp.transpose(slots_of(chosen).astype(jnp.float32), (1, 2, 0))
    combine_table = select * jnp.transpose(weight_table)[:, None, :]

    padded = jnp.pad(tokens, ((0, 8 - local_tok), (0, 0)))
    meta = jnp.pad(chosen.astype(jnp.float32), ((0, 8 - local_tok), (0, 128 - experts)))
    tok_quarter, chosen_all = quarters(padded, meta, 0)
    masks = slots_of(chosen_all[:, :, :experts].astype(jnp.int32))
    same = jnp.eye(YS, dtype=jnp.bool_)[None, :, None, :, None]
    table = jnp.transpose(masks, (2, 0, 3, 1))[:, :, :, None, :] & same
    table = table.astype(jnp.bfloat16).reshape(experts * tall, YS * 8)
    outgoing = jnp.dot(
        table, tok_quarter.reshape(YS * 8, width // YS), preferred_element_type=jnp.float32
    )
    outgoing = outgoing.astype(jnp.bfloat16).reshape(experts, tall, width // YS)
    routed = dispatch(outgoing, n_expert, 1).reshape(4 * experts * tall, width)

    contract = (((1,), (1,)), ((), ()))
    gate_act = lax.dot_general(w_gate[0], routed, contract, preferred_element_type=jnp.float32)
    up_act = lax.dot_general(w_up[0], routed, contract, preferred_element_type=jnp.float32)
    hidden = (jax.nn.silu(gate_act) * up_act).astype(jnp.bfloat16)
    hidden = gather(hidden, 2)
    hidden = hidden.reshape(w_down.shape[1], hidden.shape[2])
    summed = lax.dot_general(
        hidden, w_down[0], (((0,), (0,)), ((), ())), preferred_element_type=jnp.float32
    )
    expert_out = summed.astype(jnp.bfloat16).reshape(2, 2, experts, YS, SLOTS, feature_cols)
    expert_out = jnp.transpose(expert_out, (0, 3, 1, 2, 4, 5))
    expert_out = expert_out.reshape(n_fsdp, experts, SLOTS, feature_cols)
    returned = collect(expert_out, n_expert, n_fsdp, 3)
    mixed = jnp.einsum(
        "ect,ecd->td", combine_table, returned.astype(jnp.float32), precision=lax.Precision.HIGHEST
    )
    return mixed.astype(jnp.bfloat16)


def solution(mesh):
    placed = (
        P(("expert", "fsdp"), None),
        P(("expert", "fsdp"), None),
        P(("expert", "fsdp"), None),
        P("expert", "fsdp", None),
        P("expert", "fsdp", None),
        P("expert", None, "fsdp"),
    )
    return jax.shard_map(
        on_device,
        mesh=mesh,
        in_specs=placed,
        out_specs=P(("expert", "fsdp"), None),
        check_vma=False,
    )
```

time: 179 us -> 155 us (0.87)
  Pallas kernels: 154 us -> 143 us
  matrix products: 16.8 us -> 7.97 us
  local copies, waits for them, and re-layouts: 5.65 us -> 1.96 us
    pallas_call x2 -> x1, Pallas kernels: 67.3 us -> 22.4 us  [gather(): pl.pallas_call(gather_kernel, out_shape=jax.ShapeDtypeStruct((16,) + x.sh...]
    pallas_call x3, Pallas kernels: 86.2 us -> 120 us  [the longest x1 72.5 us: dispatch(): pl.pallas_call(functools.partial(dispatch_kernel, n), out_shape=jax.Shape...]
    reshape x2, local copies, waits for them, and re-layouts: 4.27 us -> 0.68 us  [on_device(): summed.astype(jnp.bfloat16).reshape(2, 2, experts, YS, SLOTS, feature_cols)]
    dot_general x1, matrix products: 6.22 us -> 2.72 us  [on_device(): lax.dot_general(w_gate[0], routed, contract, preferred_element_type=jnp.f...]
    dot_general x1, matrix products: 3.7 us -> 1.04 us  [on_device(): lax.dot_general(hidden, w_down[0], (((0,), (0,)), ((), ())), preferred_el...]
where the time goes in v2:
time: 155 us; the launch traced here: 154 us
  Pallas kernels  143 us (92%)
  matrix products  7.97 us (5%)
  local copies, waits for them, and re-layouts  1.96 us (1%)
  other arithmetic  1.6 us (1%)
    pallas_call x1, Pallas kernels, dispatch(): pl.pallas_call(functools.partial(dispatch_kernel, n), out_shape=jax.Shape...  72.5 us
    pallas_call x1, Pallas kernels, collect(): pl.pallas_call(functools.partial(collect_kernel, n, m), out_shape=jax.Sha...  40.7 us
    pallas_call x1, Pallas kernels, gather(): pl.pallas_call(gather_kernel, out_shape=jax.ShapeDtypeStruct((16,) + x.sh...  22.4 us
    pallas_call x1, Pallas kernels, quarters(): pl.pallas_call(quarter_kernel, out_shape=(jax.ShapeDtypeStruct((YS, rows,...  7.01 us

profile of v2, /device:TPU:1, one launch (start us, length us, event | category | flops | bytes accessed | tf_op | source)
XLA Modules:
  0.0 154.4 jit_solution(2102914160211765617)
XLA Ops:
  0.0 0.0 copy-start
  0.0 0.0 copy-start.1
  0.0 0.9 convert_reduce_fusion
  0.9 0.9 pad.8.tok_ref
  1.8 7.0 %shard_map.64 = (bf16[4,8,1024]{2,1,0:T(8,128)(2,1)S(1)}, f32[4,8,128]{2,1,0:T(8,128)S(1)}) custom-call(bf16[8,4096]{1,0:T(8,128)(2,1)S(1)} %pad.8.tok_ref, f32[8,128]{1,0:T(8,128)S(1)} %pad.9.meta_ref), custom_call_target="tpu_custom_call" | custom-call | tf_op jit(solution)/shard_map/pallas_call | solution.py:110
  8.9 0.1 copy.15
  9.0 0.1 copy.16
  9.1 0.1 compare_and_fusion
  9.2 0.2 broadcast_and_fusion
  9.4 0.2 and.55
  9.7 0.3 fusion.1.x_ref
  9.9 0.0 copy-start.4
  9.9 72.5 %shard_map.65 = bf16[4,256,4096]{2,1,0:T(8,128)(2,1)S(1)} custom-call(bf16[32,8,1024]{2,1,0:T(8,128)(2,1)S(1)} %fusion.1.x_ref), custom_call_target="tpu_custom_call" | custom-call | tf_op jit(solution)/shard_map/pallas_call | solution.py:237
  82.5 0.0 copy-done.1
  82.5 2.7 %convolution_bitcast_fusion.2 = f32[96,1024]{1,0:T(8,128)S(1)} fusion(bf16[1024,4096]{1,0:T(8,128)(2,1)S(1)} %bitcast.44, bf16[1,96,4096]{2,1,0:T(8,128)(2,1)S(1)} %copy-done.1), kind=kOutput, calls=%fused_computation.7 | convolution fusion | flops 805306368 | bytes 9568256 | tf_op jit(solution)/shard_map/dot_general | solution.py:498
  85.2 0.0 copy-done.4
  85.2 2.7 %fusion.3.x_ref = bf16[96,1024]{1,0:T(8,128)(2,1)S(1)} fusion(bf16[1024,4096]{1,0:T(8,128)(2,1)S(1)} %bitcast.45, bf16[1,96,4096]{2,1,0:T(8,128)(2,1)S(1)} %copy-done.4, f32[96,1024]{1,0:T(8,128)S(1)} %convolution_bitcast_fusion.2), kind=kOutput, calls=%fused_computation.8 | convolution fusion | flops 805896192 | bytes 9764864 | tf_op jit(solution)/shard_map/dot_general | solution.py:499
  88.0 0.0 copy-start.3
  88.0 0.0 copy-start.2
  88.0 22.4 %shard_map.66 = bf16[16,96,1024]{2,1,0:T(8,128)(2,1)S(1)} custom-call(bf16[96,1024]{1,0:T(8,128)(2,1)S(1)} %fusion.3.x_ref), custom_call_target="tpu_custom_call" | custom-call | tf_op jit(solution)/shard_map/pallas_call | solution.py:442
  110.4 0.0 copy-done
  110.4 1.0 convolution_convert_fusion
  111.5 0.2 reshape.70
  111.7 0.5 copy.17
  112.2 40.7 %shard_map.67 = bf16[32,2,4096]{2,1,0:T(2,128)(2,1)S(1)} custom-call(bf16[16,32,2,256]{3,2,1,0:T(2,128)(2,1)S(1)} %bitcast.47), custom_call_target="tpu_custom_call" | custom-call | tf_op jit(solution)/shard_map/pallas_call | solution.py:333
  152.9 0.0 copy-done.3
  152.9 0.1 reduce_sum.28
  153.0 0.1 broadcast_divide_fusion
  153.1 0.0 copy-done.2
  153.1 0.1 fusion.10
  153.2 1.2 fusion
  (9 shorter events, 0.1 us)
Async XLA Ops:
  0.0 110.4 %copy-start = (bf16[1,1536,256]{2,1,0:T(8,128)(2,1)S(1)}, bf16[1,1536,256]{2,1,0:T(8,128)(2,1)}, u32[]{:S(2)}) copy-start(bf16[1,1536,256]{2,1,0:T(8,128)(2,1)} %param.11) | copy-start | bytes 2359300
  0.0 82.5 %copy-start.1 = (bf16[1,96,4096]{2,1,0:T(8,128)(2,1)S(1)}, bf16[1,96,4096]{2,1,0:T(8,128)(2,1)}, u32[]{:S(2)}) copy-start(bf16[1,96,4096]{2,1,0:T(8,128)(2,1)} %param.9) | copy-start | bytes 2359300
  9.9 75.3 %copy-start.4 = (bf16[1,96,4096]{2,1,0:T(8,128)(2,1)S(1)}, bf16[1,96,4096]{2,1,0:T(8,128)(2,1)}, u32[]{:S(2)}) copy-start(bf16[1,96,4096]{2,1,0:T(8,128)(2,1)} %param.10) | copy-start | bytes 2359300
  88.0 64.9 %copy-start.3 = (f32[7,8]{1,0:T(8,128)S(1)}, f32[7,8]{1,0:T(8,128)}, u32[]{:S(2)}) copy-start(f32[7,8]{1,0:T(8,128)} %param.8) | copy-start | bytes 676
  88.0 65.1 %copy-start.2 = (s32[7,8]{1,0:T(8,128)S(1)}, s32[7,8]{1,0:T(8,128)}, u32[]{:S(2)}) copy-start(s32[7,8]{1,0:T(8,128)} %param.7) | copy-start | bytes 676

commit v3 on v2

--- a/solution.py
+++ b/solution.py
@@ -34,7 +34,8 @@
 
 
 def offset_of(i, n):
-    return n // 2 + ((i % 2) * 2 - 1) * ((i + 1) // 2)
+    near = i // 2 + 1
+    return near + (i % 2) * (n - 2 * near)
 
 
 def greet_all(axis, n, barrier):
@@ -266,7 +267,7 @@
         ]
 
     def column(i, target, origin):
-        g, k = i // (m - 1), i % (m - 1)
+        g, k = GROUPS - 1 - i // (m - 1), i % (m - 1)
         return pltpu.make_async_remote_copy(
             src_ref=x_ref.at[target, pl.ds(g * size, size)],
             dst_ref=place(g * size, size, origin),
@@ -308,6 +309,7 @@
         )
 
     def back_start(i, carry):
+        i = n - 2 - i
         back(i, lax.rem(e - offset_of(i, n) + n, n), e).start()
         return carry
 
@@ -320,7 +322,7 @@
 
     for g in range(GROUPS):
         lax.fori_loop(g * (m - 1), (g + 1) * (m - 1), column_land, 0)
-        lax.fori_loop(g * size, min((g + 1) * size, n - 1), back_start, 0)
+        lax.fori_loop(max(g * size - 1, 0), (g + 1) * size - 1, back_start, 0)
     own_rows = pltpu.make_async_copy(rows.at[n - 1], y_ref.at[e], own_sem.at[1])
     own_rows.start()
     lax.fori_loop(0, GROUPS * (m - 1), column_clear, 0)

time: 155 us -> 148 us (0.955)
  Pallas kernels: 143 us -> 136 us
    pallas_call x1, Pallas kernels: 72.5 us -> 63.9 us  [dispatch(): pl.pallas_call(functools.partial(dispatch_kernel, n), out_shape=jax.Shape...]
    pallas_call x1, Pallas kernels: 40.7 us -> 43.3 us  [collect(): pl.pallas_call(functools.partial(collect_kernel, n, m), out_shape=jax.Sha...]
where the time goes in v3:
time: 148 us
  Pallas kernels  136 us (92%)
  matrix products  7.97 us (5%)
  local copies, waits for them, and re-layouts  1.96 us (1%)
  other arithmetic  1.6 us (1%)
    pallas_call x1, Pallas kernels, dispatch(): pl.pallas_call(functools.partial(dispatch_kernel, n), out_shape=jax.Shape...  63.9 us
    pallas_call x1, Pallas kernels, collect(): pl.pallas_call(functools.partial(collect_kernel, n, m), out_shape=jax.Sha...  43.3 us
    pallas_call x1, Pallas kernels, gather(): pl.pallas_call(gather_kernel, out_shape=jax.ShapeDtypeStruct((16,) + x.sh...  21.7 us
    pallas_call x1, Pallas kernels, quarters(): pl.pallas_call(quarter_kernel, out_shape=(jax.ShapeDtypeStruct((YS, rows,...  7.01 us

profile of v3, /device:TPU:1, one launch (start us, length us, event | category | flops | bytes accessed | tf_op | source)
XLA Modules:
  0.0 147.6 jit_solution(4889601146737412871)
XLA Ops:
  0.0 0.0 copy-start
  0.0 0.0 copy-start.1
  0.0 0.9 convert_reduce_fusion
  0.9 0.9 pad.8.tok_ref
  1.8 7.0 %shard_map.64 = (bf16[4,8,1024]{2,1,0:T(8,128)(2,1)S(1)}, f32[4,8,128]{2,1,0:T(8,128)S(1)}) custom-call(bf16[8,4096]{1,0:T(8,128)(2,1)S(1)} %pad.8.tok_ref, f32[8,128]{1,0:T(8,128)S(1)} %pad.9.meta_ref), custom_call_target="tpu_custom_call" | custom-call | tf_op jit(solution)/shard_map/pallas_call | solution.py:111
  8.9 0.1 copy.15
  9.0 0.1 copy.16
  9.1 0.1 compare_and_fusion
  9.2 0.2 broadcast_and_fusion
  9.4 0.2 and.55
  9.7 0.3 fusion.1.x_ref
  9.9 0.0 copy-start.4
  9.9 63.9 %shard_map.65 = bf16[4,256,4096]{2,1,0:T(8,128)(2,1)S(1)} custom-call(bf16[32,8,1024]{2,1,0:T(8,128)(2,1)S(1)} %fusion.1.x_ref), custom_call_target="tpu_custom_call" | custom-call | tf_op jit(solution)/shard_map/pallas_call | solution.py:238
  73.8 0.0 copy-done.1
  73.8 2.7 %convolution_bitcast_fusion.2 = f32[96,1024]{1,0:T(8,128)S(1)} fusion(bf16[1024,4096]{1,0:T(8,128)(2,1)S(1)} %bitcast.44, bf16[1,96,4096]{2,1,0:T(8,128)(2,1)S(1)} %copy-done.1), kind=kOutput, calls=%fused_computation.7 | convolution fusion | flops 805306368 | bytes 9568256 | tf_op jit(solution)/shard_map/dot_general | solution.py:500
  76.5 0.0 copy-done.4
  76.5 2.7 %fusion.3.x_ref = bf16[96,1024]{1,0:T(8,128)(2,1)S(1)} fusion(bf16[1024,4096]{1,0:T(8,128)(2,1)S(1)} %bitcast.45, bf16[1,96,4096]{2,1,0:T(8,128)(2,1)S(1)} %copy-done.4, f32[96,1024]{1,0:T(8,128)S(1)} %convolution_bitcast_fusion.2), kind=kOutput, calls=%fused_computation.8 | convolution fusion | flops 805896192 | bytes 9764864 | tf_op jit(solution)/shard_map/dot_general | solution.py:501
  79.3 0.0 copy-start.3
  79.3 0.0 copy-start.2
  79.3 21.7 %shard_map.66 = bf16[16,96,1024]{2,1,0:T(8,128)(2,1)S(1)} custom-call(bf16[96,1024]{1,0:T(8,128)(2,1)S(1)} %fusion.3.x_ref), custom_call_target="tpu_custom_call" | custom-call | tf_op jit(solution)/shard_map/pallas_call | solution.py:444
  101.0 0.0 copy-done
  101.0 1.0 convolution_convert_fusion
  102.1 0.2 reshape.70
  102.3 0.5 copy.17
  102.8 43.3 %shard_map.67 = bf16[32,2,4096]{2,1,0:T(2,128)(2,1)S(1)} custom-call(bf16[16,32,2,256]{3,2,1,0:T(2,128)(2,1)S(1)} %bitcast.47), custom_call_target="tpu_custom_call" | custom-call | tf_op jit(solution)/shard_map/pallas_call | solution.py:335
  146.1 0.0 copy-done.3
  146.1 0.1 reduce_sum.28
  146.2 0.1 broadcast_divide_fusion
  146.3 0.0 copy-done.2
  146.3 0.1 fusion.10
  146.4 1.2 fusion
  (9 shorter events, 0.1 us)
Async XLA Ops:
  0.0 101.0 %copy-start = (bf16[1,1536,256]{2,1,0:T(8,128)(2,1)S(1)}, bf16[1,1536,256]{2,1,0:T(8,128)(2,1)}, u32[]{:S(2)}) copy-start(bf16[1,1536,256]{2,1,0:T(8,128)(2,1)} %param.11) | copy-start | bytes 2359300
  0.0 73.8 %copy-start.1 = (bf16[1,96,4096]{2,1,0:T(8,128)(2,1)S(1)}, bf16[1,96,4096]{2,1,0:T(8,128)(2,1)}, u32[]{:S(2)}) copy-start(bf16[1,96,4096]{2,1,0:T(8,128)(2,1)} %param.9) | copy-start | bytes 2359300
  9.9 66.6 %copy-start.4 = (bf16[1,96,4096]{2,1,0:T(8,128)(2,1)S(1)}, bf16[1,96,4096]{2,1,0:T(8,128)(2,1)}, u32[]{:S(2)}) copy-start(bf16[1,96,4096]{2,1,0:T(8,128)(2,1)} %param.10) | copy-start | bytes 2359300
  79.3 66.8 %copy-start.3 = (f32[7,8]{1,0:T(8,128)S(1)}, f32[7,8]{1,0:T(8,128)}, u32[]{:S(2)}) copy-start(f32[7,8]{1,0:T(8,128)} %param.8) | copy-start | bytes 676
  79.3 67.0 %copy-start.2 = (s32[7,8]{1,0:T(8,128)S(1)}, s32[7,8]{1,0:T(8,128)}, u32[]{:S(2)}) copy-start(s32[7,8]{1,0:T(8,128)} %param.7) | copy-start | bytes 676

commit v4 on v3

--- a/solution.py
+++ b/solution.py
@@ -13,6 +13,8 @@
 SLOTS = 2
 YS = 4
 GROUPS = 4
+PARTS = 8
+KSTEP = 512
 
 
 def fsdp_index(xh, y, core):
@@ -121,11 +123,15 @@
     )(tok, meta)
 
 
-def dispatch_kernel(n, x_ref, y_ref, a_send, a_recv, send_sem, recv_sem, own_sem):
+def expert_kernel(
+    n, x_ref, gate_ref, up_ref, hid_ref, routed, a_send, a_recv, t_send, t_recv, h_send, h_recv, own_sem
+):
     e = lax.axis_index("expert")
     me, xh, yy, core = fsdp_place()
     tall, quarter = x_ref.shape[1], x_ref.shape[2]
-    size = n // GROUPS
+    size = n // PARTS
+    deep = size * tall
+    cols = 4 * deep
     other = 1 - xh
     up, down, far = (yy + 1) % YS, (yy + YS - 1) % YS, (yy + 2) % YS
     to_up, to_down = fsdp_index(xh, up, core), fsdp_index(xh, down, core)
@@ -137,17 +143,18 @@
     greet_all("expert", n, barrier)
     pl.semaphore_wait(barrier, n + 3)
 
-    def place(h, y, c, first, count):
-        return y_ref.at[
+    def rows_at(h, y, c, first, count):
+        return routed.at[
             h * 2 + c,
             pl.ds(pl.multiple_of(first * tall, tall), count * tall),
             pl.ds(pl.multiple_of(y * quarter, quarter), quarter),
         ]
 
-    def hop(i, target):
+    def hop(i):
+        target = lax.rem(e + offset_of(i, n), n)
         return pltpu.make_async_remote_copy(
             src_ref=x_ref.at[target],
-            dst_ref=place(xh, yy, core, i, 1),
+            dst_ref=rows_at(xh, yy, core, i, 1),
             send_sem=a_send.at[i],
             recv_sem=a_recv.at[i],
             device_id={"expert": target},
@@ -155,100 +162,188 @@
         )
 
     def launch(i, carry):
-        hop(i, lax.rem(e + offset_of(i, n), n)).start()
+        hop(i).start()
         return carry
 
     def land(i, carry):
-        hop(i, lax.rem(e + offset_of(i, n), n)).wait_recv()
+        hop(i).wait_recv()
         return carry
 
     def clear(i, carry):
-        hop(i, lax.rem(e + offset_of(i, n), n)).wait_send()
+        hop(i).wait_send()
         return carry
 
     lax.fori_loop(0, n - 1, launch, 0)
-    own = pltpu.make_async_copy(x_ref.at[e], place(xh, yy, core, n - 1, 1), own_sem)
+    own = pltpu.make_async_copy(x_ref.at[e], rows_at(xh, yy, core, n - 1, 1), own_sem)
     own.start()
 
-    sent = []
-
-    def copy_of(h, y, c, g, target, slot):
-        block = place(h, y, c, g * size, size)
-        return pltpu.make_async_remote_copy(
-            src_ref=block,
-            dst_ref=block,
-            send_sem=send_sem.at[slot],
-            recv_sem=recv_sem.at[fsdp_index(h, y, c), g],
-            device_id={"fsdp": target},
-            device_id_type=MESH,
-        )
-
-    def send(h, y, g, *targets):
-        for target in targets:
-            copy = copy_of(h, y, core, g, target, len(sent))
-            copy.start()
-            sent.append(copy)
-
-    def arrived(h, y, c, g):
-        copy_of(h, y, c, g, to_core, 0).wait_recv()
-
-    def from_expert(g):
-        lax.fori_loop(g * size, min((g + 1) * size, n - 1), land, 0)
-        if g == GROUPS - 1:
+    class Spread:
+        def __init__(self, at, send_sem, recv_sem):
+            self.at, self.send_sem, self.recv_sem = at, send_sem, recv_sem
+
+        def copy(self, h, y, c, g, target, slot):
+            block = self.at(h, y, c, g)
+            return pltpu.make_async_remote_copy(
+                src_ref=block,
+                dst_ref=block,
+                send_sem=self.send_sem.at[g, slot],
+                recv_sem=self.recv_sem.at[fsdp_index(h, y, c), g],
+                device_id={"fsdp": target},
+                device_id_type=MESH,
+            )
+
+        def arrived(self, h, y, c, g):
+            self.copy(h, y, c, g, to_core, 0).wait_recv()
+
+        def first(self, g):
+            for slot, target in enumerate((to_x, to_up, to_down, to_core)):
+                self.copy(xh, yy, core, g, target, slot).start()
+
+        def from_x(self, g):
+            self.arrived(other, yy, core, g)
+            for slot, target in enumerate((to_up, to_down, to_core)):
+                self.copy(other, yy, core, g, target, 4 + slot).start()
+
+        def from_ring(self, h, g, slot):
+            self.arrived(h, down, core, g)
+
+            @pl.when(g % 2 == 0)
+            def _():
+                self.copy(h, down, core, g, to_up, slot).start()
+
+            self.copy(h, down, core, g, to_core, slot + 1).start()
+            self.arrived(h, up, core, g)
+
+            @pl.when(g % 2 == 1)
+            def _():
+                self.copy(h, up, core, g, to_down, slot).start()
+
+            self.copy(h, up, core, g, to_core, slot + 2).start()
+
+        def from_far(self, h, g, slot):
+            self.arrived(h, far, core, g)
+            self.copy(h, far, core, g, to_core, slot).start()
+
+        def from_core(self, g):
+            for h in (0, 1):
+                for y in range(YS):
+                    self.arrived(h, y, 1 - core, g)
+
+        def drain(self, g, carry):
+            for slot in range(15):
+                self.copy(xh, yy, core, g, to_core, slot).wait_send()
+            return carry
+
+    tokens = Spread(lambda h, y, c, g: rows_at(h, y, c, g * size, size), t_send, t_recv)
+
+    def columns(g):
+        return pl.ds(pl.multiple_of(g * cols, cols), cols)
+
+    hidden = Spread(lambda h, y, c, g: hid_ref.at[fsdp_index(h, y, c), :, columns(g)], h_send, h_recv)
+
+    def compute(g):
+        lines = gate_ref.shape[0]
+        contract = (((1,), (1,)), ((), ()))
+
+        def part(k, carry):
+            span = pl.ds(pl.multiple_of(k * KSTEP, KSTEP), KSTEP)
+            rows = routed[:, pl.ds(pl.multiple_of(g * deep, deep), deep), span]
+            rows = rows.reshape(cols, KSTEP)
+            return tuple(
+                total
+                + lax.dot_general(w[:, span], rows, contract, preferred_element_type=jnp.float32)
+                for total, w in zip(carry, (gate_ref, up_ref))
+            )
+
+        zero = jnp.zeros((lines, cols), jnp.float32)
+        gate, lift = lax.fori_loop(0, YS * quarter // KSTEP, part, (zero, zero))
+        hid_ref[me, :, columns(g)] = (jax.nn.silu(gate) * lift).astype(hid_ref.dtype)
+
+    def at_step(t, lag, action):
+        @pl.when((t >= lag) & (t < lag + PARTS))
+        def _():
+            action(t - lag)
+
+    def enter(g):
+        @pl.when(g < PARTS - 1)
+        def _():
+            lax.fori_loop(g * size, (g + 1) * size, land, 0)
+
+        @pl.when(g == PARTS - 1)
+        def _():
+            lax.fori_loop((PARTS - 1) * size, n - 1, land, 0)
             own.wait()
-        send(xh, yy, g, to_x, to_up, to_down, to_core)
-
-    def from_x(g):
-        arrived(other, yy, core, g)
-        send(other, yy, g, to_up, to_down, to_core)
-
-    def from_ring(h, g):
-        for y, onward in ((down, to_up), (up, to_down)):
-            arrived(h, y, core, g)
-            if (g % 2 == 0) == (onward is to_up):
-                send(h, y, g, onward)
-            send(h, y, g, to_core)
-
-    def from_far(h, g):
-        arrived(h, far, core, g)
-        send(h, far, g, to_core)
-
-    for step in range(GROUPS + 2):
-        if step < GROUPS:
-            from_expert(step)
-        if 1 <= step <= GROUPS:
-            from_x(step - 1)
-            from_ring(xh, step - 1)
-        if 2 <= step:
-            from_far(xh, step - 2)
-            from_ring(other, step - 2)
-    for g in range(GROUPS):
-        from_far(other, g)
-    for g in range(GROUPS):
-        for h in (0, 1):
-            for y in range(YS):
-                arrived(h, y, 1 - core, g)
+
+        tokens.first(g)
+
+    def spread_near(group, slot):
+        def action(g):
+            group.from_x(g)
+            group.from_ring(xh, g, slot)
+
+        return action
+
+    def spread_far(group, slot):
+        def action(g):
+            group.from_far(xh, g, slot)
+            group.from_ring(other, g, slot + 1)
+
+        return action
+
+    def finish(g):
+        tokens.from_far(other, g, 14)
+        tokens.from_core(g)
+        compute(g)
+        hidden.first(g)
+
+    def last(g):
+        hidden.from_far(other, g, 14)
+
+    def step(t, carry):
+        at_step(t, 0, enter)
+        at_step(t, 1, spread_near(tokens, 7))
+        at_step(t, 2, spread_far(tokens, 10))
+        at_step(t, 3, finish)
+        at_step(t, 4, spread_near(hidden, 7))
+        at_step(t, 5, spread_far(hidden, 10))
+        at_step(t, 6, last)
+        return carry
+
+    lax.fori_loop(0, PARTS + 6, step, 0)
+
+    def close(g, carry):
+        hidden.from_core(g)
+        return carry
+
+    lax.fori_loop(0, PARTS, close, 0)
     lax.fori_loop(0, n - 1, clear, 0)
-    for copy in sent:
-        copy.wait_send()
-
-
-def dispatch(x, n, number):
+    lax.fori_loop(0, PARTS, tokens.drain, 0)
+    lax.fori_loop(0, PARTS, hidden.drain, 0)
+
+
+def expert_hidden(x, w_gate, w_up, n, number):
     _, tall, quarter = x.shape
+    lines = w_gate.shape[0]
+    vmem = pl.BlockSpec(memory_space=pltpu.VMEM)
     return pl.pallas_call(
-        functools.partial(dispatch_kernel, n),
-        out_shape=jax.ShapeDtypeStruct((4, n * tall, YS * quarter), x.dtype),
-        in_specs=[ANY],
-        out_specs=ANY,
+        functools.partial(expert_kernel, n),
+        out_shape=jax.ShapeDtypeStruct((16, lines, 4 * n * tall), x.dtype),
+        in_specs=[ANY, vmem, vmem],
+        out_specs=vmem,
         scratch_shapes=[
+            pltpu.VMEM((4, n * tall, YS * quarter), x.dtype),
             DMA((n - 1,)),
             DMA((n - 1,)),
-            DMA((15 * GROUPS,)),
-            DMA((16, GROUPS)),
+            DMA((PARTS, 15)),
+            DMA((16, PARTS)),
+            DMA((PARTS, 15)),
+            DMA((16, PARTS)),
             DMA,
         ],
-        compiler_params=settings(number),
-    )(x)
+        compiler_params=pltpu.CompilerParams(
+            collective_id=number, has_side_effects=True, vmem_limit_bytes=6 * VMEM
+        ),
+    )(x, w_gate, w_up)
 
 
 def collect_kernel(n, m, x_ref, y_ref, rows, f_send, f_recv, a_send, a_recv, own_sem):
@@ -349,112 +444,6 @@
     )(x)
 
 
-def gather_kernel(x_ref, y_ref, send_sem, recv_sem, own_sem):
-    me = lax.axis_index("fsdp")
-    core, yy, xh = me % 2, (me // 2) % 4, me // 8
-    half = x_ref.shape[0] // 2
-
-    def index(h, y, c):
-        return (h * 4 + y) * 2 + c
-
-    up, down, far = (yy + 1) % 4, (yy + 3) % 4, (yy + 2) % 4
-    other = 1 - xh
-    to_up, to_down = index(xh, up, core), index(xh, down, core)
-    to_x, to_core = index(other, yy, core), index(xh, yy, 1 - core)
-
-    barrier = pltpu.get_barrier_semaphore()
-    for partner in (to_up, to_down, to_x, to_core):
-        pl.semaphore_signal(barrier, inc=1, device_id={"fsdp": partner}, device_id_type=MESH)
-    pl.semaphore_wait(barrier, 4)
-
-    sent = []
-
-    def place(block, piece):
-        return y_ref.at[block, pl.ds(piece * half, half)]
-
-    def send(block, piece, target, own=False):
-        copy = pltpu.make_async_remote_copy(
-            src_ref=x_ref.at[pl.ds(piece * half, half)] if own else place(block, piece),
-            dst_ref=place(block, piece),
-            send_sem=send_sem.at[len(sent)],
-            recv_sem=recv_sem.at[block, piece],
-            device_id={"fsdp": target},
-            device_id_type=MESH,
-        )
-        copy.start()
-        sent.append(copy)
-
-    def arrived(block, piece):
-        pltpu.make_async_remote_copy(
-            src_ref=place(block, piece),
-            dst_ref=place(block, piece),
-            send_sem=send_sem.at[0],
-            recv_sem=recv_sem.at[block, piece],
-            device_id={"fsdp": to_core},
-            device_id_type=MESH,
-        ).wait_recv()
-
-    for piece in (0, 1):
-        send(me, piece, to_x, True)
-        send(me, piece, to_up, True)
-        send(me, 1 - piece, to_down, True)
-        send(me, piece, to_core, True)
-    own = pltpu.make_async_copy(x_ref, y_ref.at[me], own_sem)
-    own.start()
-
-    def ring_first(h):
-        block = index(h, down, core)
-        arrived(block, 0)
-        send(block, 0, to_up)
-        send(block, 0, to_core)
-        block = index(h, up, core)
-        arrived(block, 1)
-        send(block, 1, to_down)
-        send(block, 1, to_core)
-
-    def ring_rest(h):
-        for block, piece in (
-            (index(h, down, core), 1),
-            (index(h, up, core), 0),
-            (index(h, far, core), 0),
-            (index(h, far, core), 1),
-        ):
-            arrived(block, piece)
-            send(block, piece, to_core)
-
-    ring_first(xh)
-    for piece in (0, 1):
-        arrived(to_x, piece)
-        send(to_x, piece, to_up)
-        send(to_x, piece, to_down)
-        send(to_x, piece, to_core)
-    ring_rest(xh)
-    ring_first(other)
-    ring_rest(other)
-    for h in (0, 1):
-        for y in range(4):
-            for piece in (0, 1):
-                arrived(index(h, y, 1 - core), piece)
-    for copy in sent:
-        copy.wait_send()
-    own.wait()
-
-
-def gather(x, number):
-    return pl.pallas_call(
-        gather_kernel,
-        out_shape=jax.ShapeDtypeStruct((16,) + x.shape, x.dtype),
-        in_specs=[pl.BlockSpec(memory_space=pltpu.VMEM)],
-        out_specs=ANY,
-        scratch_shapes=[
-            pltpu.SemaphoreType.DMA((30,)),
-            pltpu.SemaphoreType.DMA((16, 2)),
-            pltpu.SemaphoreType.DMA,
-        ],
-        compiler_params=settings(number),
-    )(x)
-
-
 def route(expert_ids, gate_scores, experts):
     weights = gate_scores / jnp.sum(gate_scores, axis=-1, keepdims=True)
     expert_iota = lax.broadcasted_iota(jnp.int32, (1, 1, experts), 2)
@@ -494,19 +483,14 @@
         table, tok_quarter.reshape(YS * 8, width // YS), preferred_element_type=jnp.float32
     )
     outgoing = outgoing.astype(jnp.bfloat16).reshape(experts, tall, width // YS)
-    routed = dispatch(outgoing, n_expert, 1).reshape(4 * experts * tall, width)
-
-    contract = (((1,), (1,)), ((), ()))
-    gate_act = lax.dot_general(w_gate[0], routed, contract, preferred_element_type=jnp.float32)
-    up_act = lax.dot_general(w_up[0], routed, contract, preferred_element_type=jnp.float32)
-    hidden = (jax.nn.silu(gate_act) * up_act).astype(jnp.bfloat16)
-    hidden = gather(hidden, 2)
+    hidden = expert_hidden(outgoing, w_gate[0], w_up[0], n_expert, 1)
     hidden = hidden.reshape(w_down.shape[1], hidden.shape[2])
     summed = lax.dot_general(
         hidden, w_down[0], (((0,), (0,)), ((), ())), preferred_element_type=jnp.float32
     )
-    expert_out = summed.astype(jnp.bfloat16).reshape(2, 2, experts, YS, SLOTS, feature_cols)
-    expert_out = jnp.transpose(expert_out, (0, 3, 1, 2, 4, 5))
+    expert_out = summed.astype(jnp.bfloat16)
+    expert_out = expert_out.reshape(PARTS, 2, 2, experts // PARTS, YS, SLOTS, feature_cols)
+    expert_out = jnp.transpose(expert_out, (1, 4, 2, 0, 3, 5, 6))
     expert_out = expert_out.reshape(n_fsdp, experts, SLOTS, feature_cols)
     returned = collect(expert_out, n_expert, n_fsdp, 3)
     mixed = jnp.einsum(

time: 148 us -> 144 us (0.973)
  matrix products: 7.97 us -> 2.5 us
  local copies, waits for them, and re-layouts: 1.96 us -> 4.21 us
    dot_general x2 -> x0, matrix products: 5.46 us -> none  [the longest x1 2.74 us: on_device(): lax.dot_general(w_up[0], routed, contract, preferred_element_type=jnp.flo...]
    pallas_call x1, Pallas kernels: 43.3 us -> 38.8 us  [collect(): pl.pallas_call(functools.partial(collect_kernel, n, m), out_shape=jax.Sha...]
    pallas_call x2 -> x1, Pallas kernels: 85.6 us -> 89.5 us  [expert_hidden(): pl.pallas_call(functools.partial(expert_kernel, n), out_shape=jax.ShapeDt...]
    unnamed x10, local copies, waits for them, and re-layouts: 0.03 us -> 2.28 us
where the time goes in v4:
time: 144 us
  Pallas kernels  135 us (94%)
  local copies, waits for them, and re-layouts  4.21 us (3%)
  matrix products  2.5 us (2%)
  other arithmetic  1.55 us (1%)
    pallas_call x1, Pallas kernels, expert_hidden(): pl.pallas_call(functools.partial(expert_kernel, n), out_shape=jax.ShapeDt...  89.5 us
    pallas_call x1, Pallas kernels, collect(): pl.pallas_call(functools.partial(collect_kernel, n, m), out_shape=jax.Sha...  38.8 us
    pallas_call x1, Pallas kernels, quarters(): pl.pallas_call(quarter_kernel, out_shape=(jax.ShapeDtypeStruct((YS, rows,...  7.01 us

profile of v4, /device:TPU:1, one launch (start us, length us, event | category | flops | bytes accessed | tf_op | source)
XLA Modules:
  0.0 143.8 jit_solution(1626975793099751143)
XLA Ops:
  0.0 0.0 copy-start
  0.0 0.8 convert_reduce_fusion
  0.9 0.9 pad.8.tok_ref
  1.8 7.0 %shard_map.64 = (bf16[4,8,1024]{2,1,0:T(8,128)(2,1)S(1)}, f32[4,8,128]{2,1,0:T(8,128)S(1)}) custom-call(bf16[8,4096]{1,0:T(8,128)(2,1)S(1)} %pad.8.tok_ref, f32[8,128]{1,0:T(8,128)S(1)} %pad.9.meta_ref), custom_call_target="tpu_custom_call" | custom-call | tf_op jit(solution)/shard_map/pallas_call | solution.py:113
  8.8 0.1 copy.15
  8.9 0.1 copy.16
  9.0 0.1 compare_and_fusion
  9.2 0.2 broadcast_and_fusion
  9.4 0.2 and.55
  9.6 0.3 fusion.1.x_ref
  9.9 0.0 copy-start.1
  9.9 1.1 copy-done.1
  11.0 0.0 copy-start.2
  11.0 1.1 copy-done.2
  12.2 89.5 %shard_map.65 = bf16[16,96,1024]{2,1,0:T(8,128)(2,1)S(1)} custom-call(bf16[32,8,1024]{2,1,0:T(8,128)(2,1)S(1)} %fusion.1.x_ref, bf16[96,4096]{1,0:T(8,128)(2,1)S(1)} %bitcast.31, bf16[96,4096]{1,0:T(8,128)(2,1)S(1)} %bitcast.32), custom_call_target="tpu_custom_call" | custom-call | tf_op jit(solution)/shard_map/pallas_call | solution.py:328
  101.7 0.0 copy-done
  101.7 1.0 convolution_convert_fusion
  102.8 0.0 copy-start.4
  102.8 0.0 copy-start.3
  102.8 0.2 reshape.66
  103.0 0.5 copy.17
  103.5 38.8 %shard_map.66 = bf16[32,2,4096]{2,1,0:T(2,128)(2,1)S(1)} custom-call(bf16[16,32,2,256]{3,2,1,0:T(2,128)(2,1)S(1)} %bitcast.30), custom_call_target="tpu_custom_call" | custom-call | tf_op jit(solution)/shard_map/pallas_call | solution.py:430
  142.3 0.0 copy-done.4
  142.3 0.1 reduce_sum.28
  142.4 0.1 broadcast_divide_fusion
  142.5 0.0 copy-done.3
  142.5 0.1 fusion.6
  142.6 1.2 fusion
  (9 shorter events, 0.1 us)
Async XLA Ops:
  0.0 101.7 %copy-start = (bf16[1,1536,256]{2,1,0:T(8,128)(2,1)S(1)}, bf16[1,1536,256]{2,1,0:T(8,128)(2,1)}, u32[]{:S(2)}) copy-start(bf16[1,1536,256]{2,1,0:T(8,128)(2,1)} %param.11) | copy-start | bytes 2359300
  9.9 1.1 copy-start.1
  11.0 1.1 copy-start.2
  102.8 39.5 %copy-start.4 = (f32[7,8]{1,0:T(8,128)S(1)}, f32[7,8]{1,0:T(8,128)}, u32[]{:S(2)}) copy-start(f32[7,8]{1,0:T(8,128)} %param.8) | copy-start | bytes 676
  102.8 39.7 %copy-start.3 = (s32[7,8]{1,0:T(8,128)S(1)}, s32[7,8]{1,0:T(8,128)}, u32[]{:S(2)}) copy-start(s32[7,8]{1,0:T(8,128)} %param.7) | copy-start | bytes 676

commit v5 on v4

--- a/solution.py
+++ b/solution.py
@@ -12,7 +12,6 @@
 DMA = pltpu.SemaphoreType.DMA
 SLOTS = 2
 YS = 4
-GROUPS = 4
 PARTS = 8
 KSTEP = 512
 
@@ -124,7 +123,29 @@
 
 
 def expert_kernel(
-    n, x_ref, gate_ref, up_ref, hid_ref, routed, a_send, a_recv, t_send, t_recv, h_send, h_recv, own_sem
+    n,
+    m,
+    x_ref,
+    gate_ref,
+    up_ref,
+    down_ref,
+    y_ref,
+    routed,
+    hid_ref,
+    stage,
+    rows,
+    a_send,
+    a_recv,
+    t_send,
+    t_recv,
+    h_send,
+    h_recv,
+    c_send,
+    c_recv,
+    b_send,
+    b_recv,
+    own_sem,
+    mine_sem,
 ):
     e = lax.axis_index("expert")
     me, xh, yy, core = fsdp_place()
@@ -138,10 +159,9 @@
     to_x, to_core = fsdp_index(other, yy, core), fsdp_index(xh, yy, 1 - core)
 
     barrier = pltpu.get_barrier_semaphore()
-    for partner in (to_up, to_down, to_x, to_core):
-        pl.semaphore_signal(barrier, inc=1, device_id={"fsdp": partner}, device_id_type=MESH)
+    greet_all("fsdp", m, barrier)
     greet_all("expert", n, barrier)
-    pl.semaphore_wait(barrier, n + 3)
+    pl.semaphore_wait(barrier, n + m - 2)
 
     def rows_at(h, y, c, first, count):
         return routed.at[
@@ -174,7 +194,7 @@
         return carry
 
     lax.fori_loop(0, n - 1, launch, 0)
-    own = pltpu.make_async_copy(x_ref.at[e], rows_at(xh, yy, core, n - 1, 1), own_sem)
+    own = pltpu.make_async_copy(x_ref.at[e], rows_at(xh, yy, core, n - 1, 1), own_sem.at[0])
     own.start()
 
     class Spread:
@@ -296,8 +316,92 @@
         compute(g)
         hidden.first(g)
 
+    width = down_ref.shape[1]
+    lines = gate_ref.shape[0]
+
+    def compute_out(g):
+        deepk = 4 * lines
+
+        def part(k, total):
+            left = hid_ref[pl.ds(k * 4, 4), :, columns(g)].reshape(deepk, cols)
+            right = down_ref[pl.ds(pl.multiple_of(k * deepk, deepk), deepk), :]
+            return total + lax.dot_general(
+                left, right, (((0,), (0,)), ((), ())), preferred_element_type=jnp.float32
+            )
+
+        out = lax.fori_loop(0, m // 4, part, jnp.zeros((cols, width), jnp.float32))
+        for b in range(4):
+            for i in range(size):
+                for y in range(YS):
+                    row = (b * size + i) * tall + y * SLOTS
+                    target = fsdp_index(b // 2, y, b % 2)
+                    stage[target, g * size + i] = out[row : row + SLOTS].astype(stage.dtype)
+
+    def column_place(g, block):
+        return rows.at[
+            pl.ds(g * size, size), :, pl.ds(pl.multiple_of(block * width, width), width)
+        ]
+
+    def column(g, k, target, origin):
+        return pltpu.make_async_remote_copy(
+            src_ref=stage.at[target, pl.ds(g * size, size)],
+            dst_ref=column_place(g, origin),
+            send_sem=c_send.at[g, k],
+            recv_sem=c_recv.at[g, k],
+            device_id={"fsdp": target},
+            device_id_type=MESH,
+        )
+
+    def mine(g):
+        return pltpu.make_async_copy(
+            stage.at[me, pl.ds(g * size, size)], column_place(g, me), mine_sem.at[g]
+        )
+
     def last(g):
         hidden.from_far(other, g, 14)
+        hidden.from_core(g)
+        compute_out(g)
+
+        def column_start(k, carry):
+            column(g, k, lax.rem(me + 1 + k, m), me).start()
+            return carry
+
+        lax.fori_loop(0, m - 1, column_start, 0)
+        mine(g).start()
+
+    def back(i, target, slot):
+        return pltpu.make_async_remote_copy(
+            src_ref=rows.at[i],
+            dst_ref=y_ref.at[slot],
+            send_sem=b_send.at[i],
+            recv_sem=b_recv.at[i],
+            device_id={"expert": target},
+            device_id_type=MESH,
+        )
+
+    own_rows = pltpu.make_async_copy(rows.at[n - 1], y_ref.at[e], own_sem.at[1])
+
+    def give_back(g):
+        def column_land(k, carry):
+            origin = lax.rem(me - 1 - k + m, m)
+            column(g, k, origin, origin).wait_recv()
+            return carry
+
+        def back_start(i, carry):
+            back(i, lax.rem(e - offset_of(i, n) + n, n), e).start()
+            return carry
+
+        lax.fori_loop(0, m - 1, column_land, 0)
+        mine(g).wait()
+
+        @pl.when(g < PARTS - 1)
+        def _():
+            lax.fori_loop(g * size, (g + 1) * size, back_start, 0)
+
+        @pl.when(g == PARTS - 1)
+        def _():
+            lax.fori_loop((PARTS - 1) * size, n - 1, back_start, 0)
+            own_rows.start()
 
     def step(t, carry):
         at_step(t, 0, enter)
@@ -307,106 +411,17 @@
         at_step(t, 4, spread_near(hidden, 7))
         at_step(t, 5, spread_far(hidden, 10))
         at_step(t, 6, last)
+        at_step(t, 7, give_back)
         return carry
 
-    lax.fori_loop(0, PARTS + 6, step, 0)
-
-    def close(g, carry):
-        hidden.from_core(g)
-        return carry
-
-    lax.fori_loop(0, PARTS, close, 0)
-    lax.fori_loop(0, n - 1, clear, 0)
-    lax.fori_loop(0, PARTS, tokens.drain, 0)
-    lax.fori_loop(0, PARTS, hidden.drain, 0)
-
-
-def expert_hidden(x, w_gate, w_up, n, number):
-    _, tall, quarter = x.shape
-    lines = w_gate.shape[0]
-    vmem = pl.BlockSpec(memory_space=pltpu.VMEM)
-    return pl.pallas_call(
-        functools.partial(expert_kernel, n),
-        out_shape=jax.ShapeDtypeStruct((16, lines, 4 * n * tall), x.dtype),
-        in_specs=[ANY, vmem, vmem],
-        out_specs=vmem,
-        scratch_shapes=[
-            pltpu.VMEM((4, n * tall, YS * quarter), x.dtype),
-            DMA((n - 1,)),
-            DMA((n - 1,)),
-            DMA((PARTS, 15)),
-            DMA((16, PARTS)),
-            DMA((PARTS, 15)),
-            DMA((16, PARTS)),
-            DMA,
-        ],
-        compiler_params=pltpu.CompilerParams(
-            collective_id=number, has_side_effects=True, vmem_limit_bytes=6 * VMEM
-        ),
-    )(x, w_gate, w_up)
-
-
-def collect_kernel(n, m, x_ref, y_ref, rows, f_send, f_recv, a_send, a_recv, own_sem):
-    e = lax.axis_index("expert")
-    me = lax.axis_index("fsdp")
-    width = x_ref.shape[3]
-    size = n // GROUPS
-    barrier = pltpu.get_barrier_semaphore()
-    greet_all("fsdp", m, barrier)
-    greet_all("expert", n, barrier)
-    pl.semaphore_wait(barrier, n + m - 2)
-
-    def place(first, count, block):
-        return rows.at[
-            pl.ds(first, count), :, pl.ds(pl.multiple_of(block * width, width), width)
-        ]
-
-    def column(i, target, origin):
-        g, k = GROUPS - 1 - i // (m - 1), i % (m - 1)
-        return pltpu.make_async_remote_copy(
-            src_ref=x_ref.at[target, pl.ds(g * size, size)],
-            dst_ref=place(g * size, size, origin),
-            send_sem=f_send.at[g, k],
-            recv_sem=f_recv.at[g, k],
-            device_id={"fsdp": target},
-            device_id_type=MESH,
-        )
-
-    def step_of(i):
-        return offset_of(i % (m - 1), m)
-
-    def column_start(i, carry):
-        column(i, lax.rem(me + step_of(i), m), me).start()
-        return carry
-
-    def column_land(i, carry):
-        origin = lax.rem(me - step_of(i) + m, m)
-        column(i, origin, origin).wait_recv()
-        return carry
-
-    def column_clear(i, carry):
-        column(i, lax.rem(me + step_of(i), m), me).wait_send()
-        return carry
-
-    own_columns = pltpu.make_async_copy(x_ref.at[me], place(0, n, me), own_sem.at[0])
-    own_columns.start()
-    lax.fori_loop(0, GROUPS * (m - 1), column_start, 0)
-    own_columns.wait()
-
-    def back(i, target, slot):
-        return pltpu.make_async_remote_copy(
-            src_ref=rows.at[i],
-            dst_ref=y_ref.at[slot],
-            send_sem=a_send.at[i],
-            recv_sem=a_recv.at[i],
-            device_id={"expert": target},
-            device_id_type=MESH,
-        )
-
-    def back_start(i, carry):
-        i = n - 2 - i
-        back(i, lax.rem(e - offset_of(i, n) + n, n), e).start()
-        return carry
+    lax.fori_loop(0, PARTS + 7, step, 0)
+
+    def column_clear(g, carry):
+        def one(k, inner):
+            column(g, k, lax.rem(me + 1 + k, m), me).wait_send()
+            return inner
+
+        return lax.fori_loop(0, m - 1, one, carry)
 
     def back_finish(i, carry):
         origin = lax.rem(e + offset_of(i, n), n)
@@ -415,33 +430,46 @@
         done.wait_send()
         return carry
 
-    for g in range(GROUPS):
-        lax.fori_loop(g * (m - 1), (g + 1) * (m - 1), column_land, 0)
-        lax.fori_loop(max(g * size - 1, 0), (g + 1) * size - 1, back_start, 0)
-    own_rows = pltpu.make_async_copy(rows.at[n - 1], y_ref.at[e], own_sem.at[1])
-    own_rows.start()
-    lax.fori_loop(0, GROUPS * (m - 1), column_clear, 0)
+    lax.fori_loop(0, n - 1, clear, 0)
+    lax.fori_loop(0, PARTS, tokens.drain, 0)
+    lax.fori_loop(0, PARTS, hidden.drain, 0)
+    lax.fori_loop(0, PARTS, column_clear, 0)
     lax.fori_loop(0, n - 1, back_finish, 0)
     own_rows.wait()
 
 
-def collect(x, n, m, number):
-    _, _, slots, width = x.shape
+def experts_round(x, w_gate, w_up, w_down, n, m, number):
+    _, tall, quarter = x.shape
+    lines = w_gate.shape[0]
+    width = YS * quarter
+    vmem = pl.BlockSpec(memory_space=pltpu.VMEM)
     return pl.pallas_call(
-        functools.partial(collect_kernel, n, m),
-        out_shape=jax.ShapeDtypeStruct((n, slots, m * width), x.dtype),
-        in_specs=[ANY],
+        functools.partial(expert_kernel, n, m),
+        out_shape=jax.ShapeDtypeStruct((n, SLOTS, width), x.dtype),
+        in_specs=[ANY, vmem, vmem, vmem],
         out_specs=ANY,
         scratch_shapes=[
-            pltpu.VMEM((n, slots, m * width), x.dtype),
-            DMA((GROUPS, m - 1)),
-            DMA((GROUPS, m - 1)),
+            pltpu.VMEM((4, n * tall, width), x.dtype),
+            pltpu.VMEM((m, lines, 4 * n * tall), x.dtype),
+            pltpu.VMEM((m, n, SLOTS, width // m), x.dtype),
+            pltpu.VMEM((n, SLOTS, width), x.dtype),
+            DMA((n - 1,)),
+            DMA((n - 1,)),
+            DMA((PARTS, 15)),
+            DMA((m, PARTS)),
+            DMA((PARTS, 15)),
+            DMA((m, PARTS)),
+            DMA((PARTS, m - 1)),
+            DMA((PARTS, m - 1)),
             DMA((n - 1,)),
             DMA((n - 1,)),
             DMA((2,)),
+            DMA((PARTS,)),
         ],
-        compiler_params=settings(number),
-    )(x)
+        compiler_params=pltpu.CompilerParams(
+            collective_id=number, has_side_effects=True, vmem_limit_bytes=8 * VMEM
+        ),
+    )(x, w_gate, w_up, w_down)
 
 
 def route(expert_ids, gate_scores, experts):
@@ -465,7 +493,6 @@
     local_tok, top_k = expert_ids.shape
     experts = n_expert
     width = tokens.shape[1]
-    feature_cols = w_down.shape[2]
     tall = YS * SLOTS
 
     chosen, weight_table = route(expert_ids, gate_scores, experts)
@@ -483,16 +510,9 @@
         table, tok_quarter.reshape(YS * 8, width // YS), preferred_element_type=jnp.float32
     )
     outgoing = outgoing.astype(jnp.bfloat16).reshape(experts, tall, width // YS)
-    hidden = expert_hidden(outgoing, w_gate[0], w_up[0], n_expert, 1)
-    hidden = hidden.reshape(w_down.shape[1], hidden.shape[2])
-    summed = lax.dot_general(
-        hidden, w_down[0], (((0,), (0,)), ((), ())), preferred_element_type=jnp.float32
+    returned = experts_round(
+        outgoing, w_gate[0], w_up[0], w_down[0], n_expert, n_fsdp, 1
     )
-    expert_out = summed.astype(jnp.bfloat16)
-    expert_out = expert_out.reshape(PARTS, 2, 2, experts // PARTS, YS, SLOTS, feature_cols)
-    expert_out = jnp.transpose(expert_out, (1, 4, 2, 0, 3, 5, 6))
-    expert_out = expert_out.reshape(n_fsdp, experts, SLOTS, feature_cols)
-    returned = collect(expert_out, n_expert, n_fsdp, 3)
     mixed = jnp.einsum(
         "ect,ecd->td", combine_table, returned.astype(jnp.float32), precision=lax.Precision.HIGHEST
     )

time: 144 us -> 128 us (0.89)
  Pallas kernels: 135 us -> 121 us
    pallas_call x2 -> x1, Pallas kernels: 128 us -> 114 us  [experts_round(): pl.pallas_call(functools.partial(expert_kernel, n, m), out_shape=jax.Shap...]
where the time goes in v5:
time: 128 us; the launch traced here: 127 us
  Pallas kernels  121 us (95%)
  local copies, waits for them, and re-layouts  3.8 us (3%)
  other arithmetic  1.47 us (1%)
  matrix products  1.47 us (1%)
    pallas_call x1, Pallas kernels, experts_round(): pl.pallas_call(functools.partial(expert_kernel, n, m), out_shape=jax.Shap...  114 us
    pallas_call x1, Pallas kernels, quarters(): pl.pallas_call(quarter_kernel, out_shape=(jax.ShapeDtypeStruct((YS, rows,...  7.01 us

profile of v5, /device:TPU:1, one launch (start us, length us, event | category | flops | bytes accessed | tf_op | source)
XLA Modules:
  0.0 127.5 jit_solution(14470187579578107358)
XLA Ops:
  0.0 0.8 convert_reduce_fusion
  0.8 0.0 copy-start
  0.8 0.0 copy-start.1
  0.8 1.0 pad.8.tok_ref
  1.8 7.0 %shard_map.64 = (bf16[4,8,1024]{2,1,0:T(8,128)(2,1)S(1)}, f32[4,8,128]{2,1,0:T(8,128)S(1)}) custom-call(bf16[8,4096]{1,0:T(8,128)(2,1)S(1)} %pad.8.tok_ref, f32[8,128]{1,0:T(8,128)S(1)} %pad.9.meta_ref), custom_call_target="tpu_custom_call" | custom-call | tf_op jit(solution)/shard_map/pallas_call | solution.py:112
  8.9 0.1 copy.13
  9.0 0.1 copy.14
  9.1 0.1 compare_and_fusion
  9.2 0.2 broadcast_and_fusion
  9.5 0.2 and.55
  9.7 0.3 fusion.1.x_ref
  9.9 0.0 copy-done
  10.0 0.0 copy-done.1
  10.0 0.0 copy-start.2
  10.0 1.1 copy-done.2
  11.1 113.6 %shard_map.65 = bf16[32,2,4096]{2,1,0:T(2,128)(2,1)S(1)} custom-call(bf16[32,8,1024]{2,1,0:T(8,128)(2,1)S(1)} %fusion.1.x_ref, bf16[96,4096]{1,0:T(8,128)(2,1)S(1)} %bitcast.22, bf16[96,4096]{1,0:T(8,128)(2,1)S(1)} %bitcast.23, bf16[1536,256]{1,0:T(8,128)(2,1)S(1)} %bitcast.24), custom_call_target="tpu_custom_call" | custom-call | tf_op jit(solution)/shard_map/pallas_call | solution.py:446
  124.7 0.0 copy-start.4
  124.7 0.7 copy-done.4
  125.4 0.1 reduce_sum.28
  125.5 0.0 copy-start.3
  125.5 0.1 broadcast_divide_fusion
  125.6 0.6 copy-done.3
  126.2 0.1 fusion.5
  126.3 1.2 fusion
  (9 shorter events, 0.1 us)
Async XLA Ops:
  0.8 9.1 %copy-start = (bf16[1,96,4096]{2,1,0:T(8,128)(2,1)S(1)}, bf16[1,96,4096]{2,1,0:T(8,128)(2,1)}, u32[]{:S(2)}) copy-start(bf16[1,96,4096]{2,1,0:T(8,128)(2,1)} %param.9) | copy-start | bytes 2359300
  0.8 9.1 %copy-start.1 = (bf16[1,96,4096]{2,1,0:T(8,128)(2,1)S(1)}, bf16[1,96,4096]{2,1,0:T(8,128)(2,1)}, u32[]{:S(2)}) copy-start(bf16[1,96,4096]{2,1,0:T(8,128)(2,1)} %param.10) | copy-start | bytes 2359300
  10.0 1.1 copy-start.2
  124.7 0.7 copy-start.4
  125.5 0.7 copy-start.3

commit v6 on v5

--- a/solution.py
+++ b/solution.py
@@ -13,7 +13,7 @@
 SLOTS = 2
 YS = 4
 PARTS = 8
-KSTEP = 512
+KSTEP = 1024
 
 
 def fsdp_index(xh, y, core):
@@ -35,8 +35,11 @@
 
 
 def offset_of(i, n):
-    near = i // 2 + 1
-    return near + (i % 2) * (n - 2 * near)
+    head = n // 4
+    beyond = (i + n - head) // n
+    place = i + beyond * (n + head - 2 - 2 * i)
+    near = place // 2 + 1
+    return near + (place % 2) * (n - 2 * near)
 
 
 def greet_all(axis, n, barrier):
@@ -510,6 +513,7 @@
         table, tok_quarter.reshape(YS * 8, width // YS), preferred_element_type=jnp.float32
     )
     outgoing = outgoing.astype(jnp.bfloat16).reshape(experts, tall, width // YS)
+    outgoing, combine_table = lax.optimization_barrier((outgoing, combine_table))
     returned = experts_round(
         outgoing, w_gate[0], w_up[0], w_down[0], n_expert, n_fsdp, 1
     )

time: 128 us -> 123 us (0.961)
  Pallas kernels: 121 us -> 117 us
  local copies, waits for them, and re-layouts: 3.8 us -> 2.25 us
    pallas_call x1, Pallas kernels: 114 us -> 110 us  [experts_round(): pl.pallas_call(functools.partial(expert_kernel, n, m), out_shape=jax.Shap...]
where the time goes in v6:
time: 123 us
  Pallas kernels  117 us (95%)
  local copies, waits for them, and re-layouts  2.25 us (2%)
  other arithmetic  2.17 us (2%)
  matrix products  1.47 us (1%)
    pallas_call x1, Pallas kernels, experts_round(): pl.pallas_call(functools.partial(expert_kernel, n, m), out_shape=jax.Shap...  110 us
    pallas_call x1, Pallas kernels, quarters(): pl.pallas_call(quarter_kernel, out_shape=(jax.ShapeDtypeStruct((YS, rows,...  7.14 us

profile of v6, /device:TPU:1, one launch (start us, length us, event | category | flops | bytes accessed | tf_op | source)
XLA Modules:
  0.0 123.1 jit_solution(345412808142969965)
XLA Ops:
  0.0 0.0 copy-start.4
  0.0 0.0 copy-start.3
  0.0 0.7 copy-done.4
  0.7 0.1 reduce_sum.28
  0.8 0.1 broadcast_divide_fusion
  0.9 0.8 fusion.5
  1.7 0.8 convert_reduce_fusion
  2.5 0.0 copy-done.3
  2.5 0.0 copy-start
  2.5 0.0 copy-start.1
  2.6 7.1 %shard_map.64 = (bf16[4,8,1024]{2,1,0:T(8,128)(2,1)S(1)}, f32[4,8,128]{2,1,0:T(8,128)S(1)}) custom-call(bf16[8,4096]{1,0:T(8,128)(2,1)S(1)} %pad.8.tok_ref, f32[8,128]{1,0:T(8,128)S(1)} %pad.9.meta_ref), custom_call_target="tpu_custom_call" | custom-call | tf_op jit(solution)/shard_map/pallas_call | solution.py:115
  9.7 0.1 copy.14
  9.9 0.1 copy.13
  10.0 0.1 compare_and_fusion
  10.1 0.2 broadcast_and_fusion
  10.3 0.2 and.53
  10.5 0.3 fusion.1.x_ref
  10.8 0.0 copy-done
  10.8 0.0 copy-done.1
  10.8 0.0 copy-start.2
  10.9 1.1 copy-done.2
  12.0 109.9 %shard_map.65 = bf16[32,2,4096]{2,1,0:T(2,128)(2,1)S(1)} custom-call(bf16[32,8,1024]{2,1,0:T(8,128)(2,1)S(1)} %fusion.1.x_ref, bf16[96,4096]{1,0:T(8,128)(2,1)S(1)} %bitcast.23, bf16[96,4096]{1,0:T(8,128)(2,1)S(1)} %bitcast.24, bf16[1536,256]{1,0:T(8,128)(2,1)S(1)} %bitcast.25), custom_call_target="tpu_custom_call" | custom-call | tf_op jit(solution)/shard_map/pallas_call | solution.py:449
  121.9 1.2 fusion
  (11 shorter events, 0.1 us)
Async XLA Ops:
  0.0 0.7 copy-start.4
  0.0 2.5 %copy-start.3 = (bf16[7,4096]{1,0:T(8,128)(2,1)S(1)}, bf16[7,4096]{1,0:T(8,128)(2,1)}, u32[]{:S(2)}) copy-start(bf16[7,4096]{1,0:T(8,128)(2,1)} %param.6) | copy-start | bytes 172036
  2.5 8.3 %copy-start = (bf16[1,96,4096]{2,1,0:T(8,128)(2,1)S(1)}, bf16[1,96,4096]{2,1,0:T(8,128)(2,1)}, u32[]{:S(2)}) copy-start(bf16[1,96,4096]{2,1,0:T(8,128)(2,1)} %param.9) | copy-start | bytes 2359300
  2.5 8.3 %copy-start.1 = (bf16[1,96,4096]{2,1,0:T(8,128)(2,1)S(1)}, bf16[1,96,4096]{2,1,0:T(8,128)(2,1)}, u32[]{:S(2)}) copy-start(bf16[1,96,4096]{2,1,0:T(8,128)(2,1)} %param.10) | copy-start | bytes 2359300
  10.8 1.1 copy-start.2
